TPU v7x, 256 devices: a whole 4x4x8 slice. The times are simulated.
256 devices in a mesh: dp: 32 (over z, x), proto: 8 (over y, core).
Axes of the slice: x: 4, y: 4, z: 8, core: 2. Of those that a mesh axis runs over, the one named last changes fastest.
Arguments:
- centroids: bfloat16 [131072, 768], P(('dp', 'proto')), may hold values from -1 to 1
- queries: bfloat16 [4096, 768], P('dp'), may hold values from -40 to 40
- positive: int32 [4096], P('dp'), may hold values from 0 to 131071
- members: bfloat16 [32, 32, 8, 16, 768], P('dp'), may hold values from -0.29882812 to 0.29882812
- member_slot: int32 [32, 32, 8, 16], P('dp'), may hold values from 0 to 511
- block_count: int32 [32, 32, 8], P('dp'), may hold values from 0 to 16, as said below
Outputs:
- concentration: float32 [131072], P(('dp', 'proto'))
- loss: float32 [4096], P('dp')
- query_grad: bfloat16 [4096, 768], P('dp')
Inputs may be any that keep to these rules, and one draw needn't show every extreme that they name: `block_count`: some block is full from every source group; the used slots come first in each block.
All inputs are finite; a program needn't handle non-finite values.
Results may differ from a plain program's by a relative error of at most 0.0056.
Values may be sent and summed in bfloat16 or wider, within the bound.
A program may use at most 128 MiB of HBM per device.

v0:
```python
import jax
import jax.numpy as jnp
from jax import lax
from jax.sharding import PartitionSpec as P


def on_device(centroids, queries, positive, members, member_slot, block_count):
    width = centroids.shape[1]
    cent_local = centroids.shape[0]
    q_local = queries.shape[0]
    column = lax.axis_index("proto")
    flat_index = lax.axis_index("dp") * lax.axis_size("proto") + column
    member_mine = lax.dynamic_index_in_dim(members, column, 2, keepdims=False)
    slot_mine = lax.dynamic_index_in_dim(member_slot, column, 2, keepdims=False)
    count_mine = lax.dynamic_index_in_dim(block_count, column, 2, keepdims=False)
    arrived, arrived_slot, arrived_count = (
        lax.all_to_all(member_mine, "dp", split_axis=1, concat_axis=0, tiled=True),
        lax.all_to_all(slot_mine, "dp", split_axis=1, concat_axis=0, tiled=True),
        lax.all_to_all(count_mine, "dp", split_axis=1, concat_axis=0, tiled=True),
    )
    slots_per = arrived.shape[2]
    member_rows = arrived.reshape(-1, width)
    slot_flat = arrived_slot.reshape(-1)
    valid = (
        (jnp.arange(slots_per, dtype=jnp.int32)[None, None, :] < arrived_count[:, :, None])
        .astype(jnp.float32)
        .reshape(-1)
    )
    picked = jnp.take(centroids, slot_flat, axis=0).astype(jnp.float32)
    distance = jnp.sqrt(jnp.sum((member_rows.astype(jnp.float32) - picked) ** 2, axis=1) + 1e-06)
    onehot = (jnp.arange(cent_local, dtype=jnp.int32)[:, None] == slot_flat[None, :]).astype(
        jnp.float32
    )
    total = jnp.dot(onehot, distance * valid, precision=lax.Precision.HIGHEST)
    counted = jnp.dot(onehot, valid, precision=lax.Precision.HIGHEST)
    concentration = (total + 1.0) / ((counted + 1.0) * jnp.log(counted + 10.0))
    inverse = 1.0 / concentration
    all_queries, all_positive = (
        lax.all_gather(queries, "dp", axis=0, tiled=True),
        lax.all_gather(positive, "dp", axis=0, tiled=True),
    )
    scores = (
        lax.dot_general(
            all_queries, centroids, (((1,), (1,)), ((), ())), preferred_element_type=jnp.float32
        )
        * inverse[None, :]
    )
    local_positive = all_positive - flat_index * cent_local
    positive_hit = (
        jnp.arange(cent_local, dtype=jnp.int32)[None, :] == local_positive[:, None]
    ).astype(jnp.float32)
    target_part = jnp.sum(scores * positive_hit, axis=1)
    local_max = jnp.max(scores, axis=1)
    row_max = lax.pmax(local_max, ("dp", "proto"))
    local_sum = jnp.sum(jnp.exp(scores - row_max[:, None]), axis=1)
    row_sum, target = lax.psum((local_sum, target_part), ("dp", "proto"))
    loss_all = row_max + jnp.log(row_sum) - target
    loss_mine = lax.dynamic_slice_in_dim(loss_all, lax.axis_index("dp") * q_local, q_local)
    probs = jnp.exp(scores - row_max[:, None]) / row_sum[:, None]
    weight = ((probs - positive_hit) * inverse[None, :]).astype(jnp.bfloat16)
    partial_rows = lax.psum_scatter(
        jnp.dot(weight, centroids, preferred_element_type=jnp.float32),
        "dp",
        scatter_dimension=0,
        tiled=True,
    )
    summed = lax.psum(partial_rows, "proto")
    return (concentration, loss_mine, summed.astype(jnp.bfloat16))


def solution(mesh):
    placed = (
        P(("dp", "proto"), None),
        P("dp", None),
        P("dp"),
        P("dp", None, None, None, None),
        P("dp", None, None, None),
        P("dp", None, None),
    )
    return jax.shard_map(
        on_device,
        mesh=mesh,
        in_specs=placed,
        out_specs=(P(("dp", "proto")), P("dp"), P("dp", None)),
        check_vma=False,
    )
```

profile of v0, /device:TPU:1, one launch (start us, length us, event | category | flops | bytes accessed | tf_op | source)
XLA Modules:
  0.0 547.5 jit_solution(13499479848178516080)
XLA Ops:
  7.2 0.0 copy-start
  7.2 0.0 all-gather.3.cloned.1.call-start
  7.2 0.7 all-gather.3.cloned.1.call-update
  7.9 0.7 constant_dynamic-slice_fusion
  8.6 0.7 copy.28
  9.3 11.9 %all-to-all-start.1 = ((s32[1,32,1]{2,0,1:T(1,128)}), s32[1,32,1]{2,0,1:T(1,128)S(1)}, u32[]{:S(2)}, u32[]{:S(2)}) async-start(s32[1,32,1]{2,0,1:T(1,128)} %copy.28), calls=%async_computation.1 | async-start | bytes 32768 | tf_op jit(solution)/shard_map/all_to_all | solution.py:19
  21.2 0.7 constant_dynamic-slice_fusion.1
  21.9 0.7 copy.23
  22.5 7.2 %all-to-all-done.1 = s32[1,32,1]{2,0,1:T(1,128)S(1)} async-done(((s32[1,32,1]{2,0,1:T(1,128)}), s32[1,32,1]{2,0,1:T(1,128)S(1)}, u32[]{:S(2)}, u32[]{:S(2)}) %all-to-all-start.1) | async-done | bytes 160 | tf_op jit(solution)/shard_map/all_to_all | solution.py:19
  29.7 3.8 all-to-all-start
  33.5 2.1 dynamic-slice_bitcast_fusion
  35.6 6.5 %all-to-all-done = s32[1,32,16]{2,0,1:T(1,128)S(1)} async-done(((s32[1,32,16]{2,0,1:T(1,128)}), s32[1,32,16]{2,0,1:T(1,128)S(1)}, u32[]{:S(2)}, u32[]{:S(2)}) %all-to-all-start) | async-done | bytes 2080 | tf_op jit(solution)/shard_map/all_to_all | solution.py:18
  42.1 3.9 all-to-all-start.2
  46.0 0.0 reduce-scatter.2.cloned.1.call-start
  46.1 48.1 %all-gather = s32[32,1,128]{2,1,0:T(1,128)S(1)} all-gather(s32[1,1,128]{2,1,0:T(1,128)} %bitcast.42), channel_id=1, replica_groups=mesh['dp'=32,'proto'=8] {'dp'}, dimensions={0}, use_global_device_ids=true | all-gather | bytes 16896 | tf_op jit(solution)/shard_map/all_gather | solution.py:40
  94.2 0.7 reduce.4
  94.9 0.1 iota_compare_fusion.4
  95.0 0.1 lt.61
  95.1 0.1 reshape.139
  95.1 0.1 reshape.124
  95.2 0.5 broadcast.91
  95.8 0.7 reduce.9
  96.4 0.1 eq.31
  96.5 0.1 copy.25
  96.6 0.1 copy.26
  96.7 0.0 copy-done
  96.7 2.0 gather_fusion
  98.8 0.3 fusion.2
  99.1 0.0 all-to-all-done.2
  99.1 0.5 multiply_reduce_fusion.1
  99.6 0.1 sqrt.7
  99.7 0.6 fusion.3
  100.2 0.6 add_divide_fusion
  100.8 2.9 all-gather.3.cloned.1.call-done
  103.7 8.4 %multiply_reduce_fusion = (f32[4096]{0:T(1024)S(1)}, f32[4096,512]{0,1:T(8,128)}) fusion(f32[512]{0:T(512)S(1)} %get-tuple-element.7, bf16[4096,768]{1,0:T(8,128)(2,1)} %all-gather.3.cloned.1.call-done, bf16[512,768]{1,0:T(8,128)(2,1)S(1)} %copy-done), kind=kOutput, calls=%fused_computation.6 | convolution fusion | flops 3225415680 | bytes 15484928 | tf_op jit(solution)/shard_map/dot_general | solution.py:43
  112.1 76.3 %pmax.7 = f32[4096]{0:T(1024)S(1)} all-reduce(f32[4096]{0:T(1024)S(1)} %get-tuple-element.9), channel_id=1, replica_groups=mesh['dp'=32,'proto'=8] {'dp','proto'}, use_global_device_ids=true, to_apply=%region_2.3 | all-reduce | flops 4096 | bytes 32768 | tf_op jit(solution)/shard_map/pmax | solution.py:54
  188.4 5.0 fusion
  193.4 74.0 %all-reduce = (f32[4096]{0:T(1024)S(1)}, f32[4096]{0:T(1024)S(1)}) all-reduce(f32[4096]{0:T(1024)S(1)} %get-tuple-element.4, f32[4096]{0:T(1024)S(1)} %get-tuple-element.3), channel_id=1, replica_groups=mesh['dp'=32,'proto'=8] {'dp','proto'}, use_global_device_ids=true, to_apply=%region_6.7 | all-reduce | flops 8192 | bytes 65536 | tf_op jit(solution)/shard_map/psum | solution.py:56
  267.4 13.1 %fusion.1 = f32[4096,768]{1,0:T(8,128)} fusion(bf16[512,768]{1,0:T(8,128)(2,1)S(1)} %copy-done, f32[4096,512]{0,1:T(8,128)} %get-tuple-element.10, f32[4096]{0:T(1024)S(1)} %get-tuple-element.6, s32[4096]{0:T(1024)S(1)} %bitcast.36, f32[4096]{0:T(1024)S(1)} %pmax.7, f32[512]{0:T(512)S(1)} %get-tuple-element.7), kind=kOutput, calls=%fused_computation.7 | convolution fusion | flops 3238002688 | bytes 21809152 | tf_op jit(solution)/shard_map/dot_general | solution.py:62
  280.5 0.0 reduce-scatter.2.cloned.1.call-update
  280.5 0.6 dynamic-slice_subtract_fusion
  281.1 229.7 %reduce-scatter.2.cloned.1.call-done = f32[128,768]{1,0:T(8,128)} async-done(((f32[4096,768]{1,0:T(8,128)}), f32[128,768]{1,0:T(8,128)}) %reduce-scatter.2.cloned.1.call-update) | async-done | bytes 393232 | tf_op jit(solution)/shard_map/reduce_scatter | solution.py:61
  510.8 29.9 %all-reduce.2 = bf16[128,768]{1,0:T(8,128)(2,1)} all-reduce(f32[128,768]{1,0:T(8,128)} %reduce-scatter.2.cloned.1.call-done), channel_id=1, replica_groups=mesh['dp'=32,'proto'=8] {'proto'}, use_global_device_ids=true, to_apply=%region_8.9 | all-reduce | flops 98304 | bytes 589824 | tf_op jit(solution)/shard_map/psum | solution.py:67
  (6 shorter events, 0.0 us)
Async XLA Ops:
  7.2 89.6 %copy-start = (bf16[512,768]{1,0:T(8,128)(2,1)S(1)}, bf16[512,768]{1,0:T(8,128)(2,1)}, u32[]{:S(2)}) copy-start(bf16[512,768]{1,0:T(8,128)(2,1)} %param.6) | copy-start | bytes 2359300
  7.2 96.6 %all-gather.3.cloned.1.call-start = ((), (), s32[]{:S(2)}) async-start(), calls=%async_computation.4 | async-start | bytes 6488064 | tf_op jit(solution)/shard_map/all_gather | solution.py:39
  9.3 20.4 %all-to-all-start.1 = ((s32[1,32,1]{2,0,1:T(1,128)}), s32[1,32,1]{2,0,1:T(1,128)S(1)}, u32[]{:S(2)}, u32[]{:S(2)}) async-start(s32[1,32,1]{2,0,1:T(1,128)} %copy.28), calls=%async_computation.1 | async-start | bytes 32768 | tf_op jit(solution)/shard_map/all_to_all | solution.py:19
  29.7 12.4 %all-to-all-start = ((s32[1,32,16]{2,0,1:T(1,128)}), s32[1,32,16]{2,0,1:T(1,128)S(1)}, u32[]{:S(2)}, u32[]{:S(2)}) async-start(s32[1,32,16]{2,0,1:T(1,128)} %bitcast), calls=%async_computation | async-start | bytes 32768 | tf_op jit(solution)/shard_map/all_to_all | solution.py:18
  42.1 56.9 %all-to-all-start.2 = ((bf16[1,32,16,768]{3,2,0,1:T(8,128)(2,1)}), bf16[1,32,16,768]{3,2,0,1:T(8,128)(2,1)S(1)}, u32[]{:S(2)}, u32[]{:S(2)}) async-start(bf16[1,32,16,768]{3,2,0,1:T(8,128)(2,1)} %dynamic-slice_bitcast_fusion), calls=%async_computation.2 | async-start | bytes 1572864 | tf_op jit(solution)/shard_map/all_to_all | solution.py:17
  46.0 464.7 %reduce-scatter.2.cloned.1.call-start = ((), (), s32[]{:S(2)}) async-start(), calls=%async_computation.5 | async-start | bytes 12976128 | tf_op jit(solution)/shard_map/reduce_scatter | solution.py:61
Sparse Core Ops, SparseCore 0:
  10.6 93.1 all-gather.2
  280.6 230.1 reduce-scatter.1
where the time goes:
time: 550 us; the launch traced here: 548 us
  waiting for transfers between devices  247 us (45%)
  blocking collectives  228 us (41%)
  matrix products  22.3 us (4%)
  starting transfers between devices  19.6 us (4%)
  between operations  14.2 us (3%)
  other arithmetic  8.13 us (1%)
  local copies, waits for them, and re-layouts  7.99 us (1%)
    reduce_scatter x1, waiting for transfers between devices, on_device(): lax.psum_scatter(jnp.dot(weight, centroids, preferred_element_type=jnp.fl...  230 us
    pmax x1, blocking collectives, on_device(): row_max = lax.pmax(local_max, ('dp', 'proto'))  76.3 us
    psum x1, blocking collectives, on_device(): row_sum, target = lax.psum((local_sum, target_part), ('dp', 'proto'))  74 us
    all_gather x1, blocking collectives, on_device(): lax.all_gather(positive, 'dp', axis=0, tiled=True)  48.1 us
    psum x1, blocking collectives, on_device(): summed = lax.psum(partial_rows, 'proto')  29.9 us
    dot_general x1, matrix products, on_device(): jnp.dot(weight, centroids, preferred_element_type=jnp.float32)  13.1 us
    all_to_all x1, starting transfers between devices, on_device(): lax.all_to_all(count_mine, 'dp', split_axis=1, concat_axis=0, tiled=True)  11.9 us
  transfers between devices with their start and end apart: 5, of which 4 were waited for; matrix products, arithmetic and copies ran while one was open for 2% of the time, Pallas kernels for 0%

commit v1 on v0

v1 whole, which is shorter than its diff:
```python
import functools

import jax
import jax.numpy as jnp
from jax import lax
from jax.experimental import pallas as pl
from jax.experimental.pallas import tpu as pltpu
from jax.sharding import PartitionSpec as P

MESH = pl.DeviceIdType.MESH
NX, NZ, NP = 4, 8, 8
ROWS, WIDTH, CENT = 16, 768, 512
QS = NX * NZ * ROWS
F32, BF16 = jnp.float32, jnp.bfloat16


def remote(src, dst, send, recv, device):
    return pltpu.make_async_remote_copy(
        src_ref=src, dst_ref=dst, send_sem=send, recv_sem=recv, device_id=device, device_id_type=MESH
    )


def columns_of(rows):
    n = rows.shape[0]
    wide = jnp.broadcast_to(rows, (n, ROWS, 128))
    lane = lax.broadcasted_iota(jnp.int32, (n, ROWS, 128), 2)
    sub = lax.broadcasted_iota(jnp.int32, (n, ROWS, 128), 1)
    return jnp.sum(jnp.where(lane == sub, wide, 0.0), axis=2, keepdims=True).reshape(n * ROWS, 1)


def kernel(
    cent, qry, mem, slot, pos, conc_o, loss_o, grad_o,
    call, qall, pall, mx, mall, slx, sall, invall, score, stats, sxb, szb, colr, posb,
    gsend, grx, hsend, hz, acc, fin, lfin,
    local, mx_s, mx_r, sx_s, sx_r, mz_s, mz_r, sz_s, sz_r, qz_s, qz_r, qx_s, qx_r, pz_s, pz_r, px_s, px_r,
    cy_s, cy_r, cc_s, cc_r, iv_s, iv_r, tx_s, tx_r, tz_s, tz_r, gx_s, gx_r, gz_s, gz_r, fn_s, fn_r, ln_s, ln_r,
):
    dp = lax.axis_index("dp")
    p = lax.axis_index("proto")
    z, x = dp // NX, dp % NX
    y, c = p // 2, p % 2

    def at_x(d):
        return (x + d) % NX

    def at_z(d):
        return (z + d) % NZ

    def at_p(d):
        return (p + d) % NP

    def dev_x(d):
        return {"dp": z * NX + at_x(d), "proto": p}

    def dev_z(d):
        return {"dp": at_z(d) * NX + x, "proto": p}

    def dev_p(q):
        return {"dp": dp, "proto": q}

    barrier = pltpu.get_barrier_semaphore()
    for d in range(1, NX):
        pl.semaphore_signal(barrier, inc=1, device_id=dev_x(d), device_id_type=MESH)
    for d in range(1, NZ):
        pl.semaphore_signal(barrier, inc=1, device_id=dev_z(d), device_id_type=MESH)
    for d in range(1, NP):
        pl.semaphore_signal(barrier, inc=1, device_id=dev_p(at_p(d)), device_id_type=MESH)
    pl.semaphore_wait(barrier, NX + NZ + NP - 3)

    sends = []

    def go(copy):
        copy.start()
        sends.append(copy)

    z_order = (4, 3, 5, 2, 6, 1, 7)
    half = CENT // 2
    top, bottom = pl.ds(0, half), pl.ds(half, half)
    up = ((y + 1) % 4) * 2 + c
    down = ((y + 3) % 4) * 2 + c
    far = ((y + 2) % 4) * 2 + c
    mate = y * 2 + (1 - c)

    for d in z_order:
        go(remote(qry.at[p], qall.at[x, z], qz_s.at[d - 1], qz_r.at[d - 1], dev_z(d)))
        go(remote(pos, pall.at[x, z], pz_s.at[d - 1], pz_r.at[d - 1], dev_z(d)))
    go(remote(cent.at[top], call.at[p, top], cy_s.at[0], cy_r.at[0], dev_p(up)))
    go(remote(cent.at[bottom], call.at[p, bottom], cy_s.at[3], cy_r.at[3], dev_p(down)))
    go(remote(cent.at[bottom], call.at[p, bottom], cy_s.at[1], cy_r.at[1], dev_p(up)))
    go(remote(cent.at[top], call.at[p, top], cy_s.at[2], cy_r.at[2], dev_p(down)))
    go(remote(cent, call.at[p], cc_s.at[0], cc_r.at[0], dev_p(mate)))
    for d in (2, 1, 3):
        go(remote(mem.at[:, at_x(d), p], mx.at[d - 1], mx_s.at[d - 1], mx_r.at[d - 1], dev_x(d)))
        go(remote(slot.at[:, at_x(d)], slx.at[d - 1], sx_s.at[d - 1], sx_r.at[d - 1], dev_x(d)))
    for d in z_order:
        go(remote(mem.at[at_z(d), x, p], mall.at[z, 0], mz_s.at[0, d - 1], mz_r.at[0, d - 1], dev_z(d)))
        go(remote(slot.at[at_z(d), x], sall.at[z, 0], sz_s.at[0, d - 1], sz_r.at[0, d - 1], dev_z(d)))
    own = (
        pltpu.make_async_copy(cent, call.at[p], local.at[0]),
        pltpu.make_async_copy(qry.at[p], qall.at[x, z], local.at[1]),
        pltpu.make_async_copy(mem.at[z, x, p], mall.at[z, 0], local.at[2]),
    )
    for copy in own:
        copy.start()
    pall[x, z] = pos[...]
    sall[z, 0] = slot[z, x]
    own[1].wait()

    for d in range(1, NZ):
        src = at_z(NZ - d)
        remote(qry.at[p], qall.at[x, src], qz_s.at[d - 1], qz_r.at[d - 1], dev_z(d)).wait_recv()
        remote(pos, pall.at[x, src], pz_s.at[d - 1], pz_r.at[d - 1], dev_z(d)).wait_recv()
    for d in (2, 1, 3):
        go(remote(qall.at[x], qall.at[x], qx_s.at[d - 1], qx_r.at[d - 1], dev_x(d)))
        go(remote(pall.at[x], pall.at[x], px_s.at[d - 1], px_r.at[d - 1], dev_x(d)))

    def members_on(d):
        remote(mem.at[:, x, p], mx.at[d - 1], mx_s.at[d - 1], mx_r.at[d - 1], dev_x(d)).wait_recv()
        remote(slot.at[:, x], slx.at[d - 1], sx_s.at[d - 1], sx_r.at[d - 1], dev_x(d)).wait_recv()
        for e in z_order:
            go(remote(mx.at[d - 1, at_z(e)], mall.at[z, d], mz_s.at[d, e - 1], mz_r.at[d, e - 1], dev_z(e)))
            go(remote(slx.at[d - 1, at_z(e)], sall.at[z, d], sz_s.at[d, e - 1], sz_r.at[d, e - 1], dev_z(e)))
        mall[z, d] = mx[d - 1, z]
        sall[z, d] = slx[d - 1, z]

    members_on(1)
    members_on(3)
    remote(cent.at[top], call.at[down, top], cy_s.at[0], cy_r.at[0], dev_p(up)).wait_recv()
    go(remote(call.at[down, top], call.at[down, top], cy_s.at[4], cy_r.at[4], dev_p(up)))
    remote(cent.at[bottom], call.at[up, bottom], cy_s.at[3], cy_r.at[3], dev_p(down)).wait_recv()
    go(remote(call.at[up, bottom], call.at[up, bottom], cy_s.at[5], cy_r.at[5], dev_p(down)))
    members_on(2)

    for d in range(1, NX):
        src = at_x(NX - d)
        remote(qall.at[x], qall.at[src], qx_s.at[d - 1], qx_r.at[d - 1], dev_x(d)).wait_recv()
        remote(pall.at[x], pall.at[src], px_s.at[d - 1], px_r.at[d - 1], dev_x(d)).wait_recv()
    base = (dp * (NP * CENT)).astype(F32)
    posb[...] = jnp.broadcast_to(columns_of(pall[...].reshape(NX * NZ, 1, 128)) - base, (QS, 128))

    def scores(chunk):
        def rows(i, carry):
            r = pl.ds(i * 2, 2)
            q = qall[r].reshape(2 * NZ * ROWS, WIDTH)
            score[chunk, pl.ds(i * 256, 256), :] = lax.dot_general(
                q, call[chunk], (((1,), (1,)), ((), ())), preferred_element_type=F32
            )
            return carry

        lax.fori_loop(0, 2, rows, 0)

    own[0].wait()
    scores(p)
    remote(cent, call.at[mate], cc_s.at[0], cc_r.at[0], dev_p(mate)).wait_recv()
    scores(mate)
    remote(cent.at[bottom], call.at[down, bottom], cy_s.at[1], cy_r.at[1], dev_p(up)).wait_recv()
    go(remote(call.at[down], call.at[down], cc_s.at[1], cc_r.at[1], dev_p(mate)))
    remote(cent.at[top], call.at[up, top], cy_s.at[2], cy_r.at[2], dev_p(down)).wait_recv()
    go(remote(call.at[up], call.at[up], cc_s.at[2], cc_r.at[2], dev_p(mate)))
    flip = 1 - 2 * c
    scores(down)
    scores(up)
    remote(call.at[down], call.at[down + flip], cc_s.at[1], cc_r.at[1], dev_p(mate)).wait_recv()
    scores(down + flip)
    remote(call.at[up], call.at[up + flip], cc_s.at[2], cc_r.at[2], dev_p(mate)).wait_recv()
    scores(up + flip)

    own[2].wait()
    for e in range(1, NZ):
        src = at_z(NZ - e)
        for d in range(NX):
            remote(mem.at[z, x, p], mall.at[src, d], mz_s.at[d, e - 1], mz_r.at[d, e - 1], dev_z(e)).wait_recv()
            remote(slot.at[z, x], sall.at[src, d], sz_s.at[d, e - 1], sz_r.at[d, e - 1], dev_z(e)).wait_recv()
    which = columns_of(sall[...].reshape(NX * NZ, 1, 128))
    cluster = lax.broadcasted_iota(jnp.int32, (QS, CENT), 1).astype(F32)
    hot = which == cluster
    picked = jnp.dot(hot.astype(BF16), call[p], preferred_element_type=F32)
    gap = mall[...].reshape(QS, WIDTH).astype(F32) - picked
    dist = jnp.sqrt(jnp.sum(gap * gap, axis=1, keepdims=True) + 1e-06)
    total = jnp.sum(jnp.where(hot, dist, 0.0), axis=0, keepdims=True)
    count = jnp.sum(hot.astype(F32), axis=0, keepdims=True)
    conc = (total + 1.0) / ((count + 1.0) * jnp.log(count + 10.0))
    conc_o[...] = conc
    invall[p] = 1.0 / conc
    for d in (4, 3, 5, 2, 6, 1, 7):
        go(remote(invall.at[p], invall.at[p], iv_s.at[d - 1], iv_r.at[d - 1], dev_p(at_p(d))))

    remote(call.at[down, top], call.at[far, top], cy_s.at[4], cy_r.at[4], dev_p(up)).wait_recv()
    remote(call.at[up, bottom], call.at[far, bottom], cy_s.at[5], cy_r.at[5], dev_p(down)).wait_recv()
    go(remote(call.at[far], call.at[far], cc_s.at[3], cc_r.at[3], dev_p(mate)))
    scores(far)
    remote(call.at[far], call.at[far + flip], cc_s.at[3], cc_r.at[3], dev_p(mate)).wait_recv()
    scores(far + flip)
    for d in range(1, NP):
        src = at_p(NP - d)
        remote(invall.at[p], invall.at[src], iv_s.at[d - 1], iv_r.at[d - 1], dev_p(src)).wait_recv()

    step = 16
    lane = lax.broadcasted_iota(jnp.int32, (step, 128), 1)

    def soft(i, carry):
        r = pl.ds(pl.multiple_of(i * step, step), step)
        best = None
        for k in range(NP):
            zed = score[k, r, :] * invall[k]
            score[k, r, :] = zed
            best = zed if best is None else jnp.maximum(best, zed)
        top_z = jnp.max(best, axis=1, keepdims=True)
        here = posb[r, 0:1]
        col = lax.broadcasted_iota(jnp.int32, (step, CENT), 1).astype(F32)
        added, hits = None, None
        for k in range(NP):
            zed = score[k, r, :]
            hit = jnp.where(col == here - float(k * CENT), zed, 0.0)
            e = jnp.exp(zed - top_z)
            score[k, r, :] = e
            added = e if added is None else added + e
            hits = hit if hits is None else hits + hit
        summed = jnp.sum(added, axis=1, keepdims=True)
        target = jnp.sum(hits, axis=1, keepdims=True)
        stats[r, :] = jnp.where(lane == 0, top_z, jnp.where(lane == 1, summed, target))
        return carry

    lax.fori_loop(0, QS // step, soft, 0)

    mine = stats[...].T[0:8, :]
    sxb[x] = mine

    def merged(ref, n):
        best = ref[0][0:1, :]
        for k in range(1, n):
            best = jnp.maximum(best, ref[k][0:1, :])
        added, target = None, None
        for k in range(n):
            part = ref[k][1:2, :] * jnp.exp(ref[k][0:1, :] - best)
            added = part if added is None else added + part
            target = ref[k][2:3, :] if target is None else target + ref[k][2:3, :]
        return best, added, target

    for d in (2, 1, 3):
        go(remote(sxb.at[x], sxb.at[x], tx_s.at[d - 1], tx_r.at[d - 1], dev_x(d)))
    for d in range(1, NX):
        src = at_x(NX - d)
        remote(sxb.at[x], sxb.at[src], tx_s.at[d - 1], tx_r.at[d - 1], dev_x(d)).wait_recv()
    best, added, target = merged(sxb, NX)
    szb[z] = jnp.concatenate([best, added, target, jnp.zeros((5, QS), F32)], axis=0)
    for d in z_order:
        go(remote(szb.at[z], szb.at[z], tz_s.at[d - 1], tz_r.at[d - 1], dev_z(d)))
    for d in range(1, NZ):
        src = at_z(NZ - d)
        remote(szb.at[z], szb.at[src], tz_s.at[d - 1], tz_r.at[d - 1], dev_z(d)).wait_recv()
    best, added, target = merged(szb, NZ)
    share = jnp.exp(mine[0:1, :] - best) / added
    loss = best + jnp.log(added) - target
    colr[...] = jnp.concatenate([share, loss, jnp.zeros((126, QS), F32)], axis=0).T

    def part(block):
        rows = pl.ds(pl.multiple_of(block * (NZ * ROWS), NZ * ROWS), NZ * ROWS)
        scale = colr[rows, 0:1]
        here = posb[rows, 0:1]
        col = lax.broadcasted_iota(jnp.int32, (NZ * ROWS, CENT), 1).astype(F32)
        acc[...] = jnp.zeros_like(acc)

        def add(k, carry):
            hit = (col == here - (k * CENT).astype(F32)).astype(F32)
            w = ((score[k, rows, :] * scale - hit) * invall[k]).astype(BF16)
            acc[...] += jnp.dot(w, call[k], preferred_element_type=F32)
            return carry

        lax.fori_loop(0, NP, add, 0)

    for d in (2, 1, 3):
        part(at_x(d))
        gsend[d - 1] = acc[...].astype(BF16).reshape(NZ, ROWS, WIDTH)
        go(remote(gsend.at[d - 1], grx.at[d - 1], gx_s.at[d - 1], gx_r.at[d - 1], dev_x(d)))
    part(x)
    for d in (1, 3, 2):
        remote(gsend.at[d - 1], grx.at[d - 1], gx_s.at[d - 1], gx_r.at[d - 1], dev_x(d)).wait_recv()
    summed = acc[...] + (
        grx[0].reshape(NZ * ROWS, WIDTH).astype(F32)
        + grx[1].reshape(NZ * ROWS, WIDTH).astype(F32)
        + grx[2].reshape(NZ * ROWS, WIDTH).astype(F32)
    )
    acc[...] = summed
    hsend[...] = summed.astype(BF16).reshape(NZ, ROWS, WIDTH)
    for d in z_order:
        go(remote(hsend.at[at_z(d)], hz.at[d - 1], gz_s.at[d - 1], gz_r.at[d - 1], dev_z(d)))
    grad = acc[pl.ds(pl.multiple_of(z * ROWS, ROWS), ROWS), :]
    for d in range(1, NZ):
        remote(hsend.at[z], hz.at[d - 1], gz_s.at[d - 1], gz_r.at[d - 1], dev_z(d)).wait_recv()
        grad = grad + hz[d - 1].astype(F32)

    fin[p] = grad.astype(BF16)
    lfin[p] = colr[pl.ds(pl.multiple_of((x * NZ + z) * ROWS, ROWS), ROWS), :]
    for d in (4, 3, 5, 2, 6, 1, 7):
        go(remote(fin.at[p], fin.at[p], fn_s.at[d - 1], fn_r.at[d - 1], dev_p(at_p(d))))
        go(remote(lfin.at[p], lfin.at[p], ln_s.at[d - 1], ln_r.at[d - 1], dev_p(at_p(d))))
    for d in range(1, NP):
        src = at_p(NP - d)
        remote(fin.at[p], fin.at[src], fn_s.at[d - 1], fn_r.at[d - 1], dev_p(src)).wait_recv()
        remote(lfin.at[p], lfin.at[src], ln_s.at[d - 1], ln_r.at[d - 1], dev_p(src)).wait_recv()
    grad_o[...] = fin[...].reshape(NP * ROWS, WIDTH)
    loss_o[...] = lfin[...].reshape(NP * ROWS, 128).T[1:2, :]
    for copy in sends:
        copy.wait_send()


def on_device(centroids, queries, positive, members, member_slot, block_count):
    column = lax.axis_index("proto")
    slot_mine = lax.dynamic_index_in_dim(member_slot[0], column, 1, keepdims=False)
    count_mine = lax.dynamic_index_in_dim(block_count[0], column, 1, keepdims=False)
    used = jnp.arange(ROWS, dtype=jnp.int32)[None, :] < count_mine[:, None]
    slot = jnp.where(used, slot_mine, -1).astype(F32)
    slot = jnp.pad(slot, ((0, 0), (0, 128 - ROWS))).reshape(NZ, NX, 1, 128)
    pos = lax.dynamic_slice_in_dim(positive, column * ROWS, ROWS).astype(F32)
    pos = jnp.pad(pos, (0, 128 - ROWS)).reshape(1, 128)
    vmem = pltpu.VMEM
    dma = pltpu.SemaphoreType.DMA
    sems = []
    for shape in (
        (NX - 1,), (NX - 1,), (NX, NZ - 1), (NX, NZ - 1), (NZ - 1,), (NX - 1,), (NZ - 1,), (NX - 1,),
        (6,), (4,), (NP - 1,), (NX - 1,), (NZ - 1,), (NX - 1,), (NZ - 1,), (NP - 1,), (NP - 1,),
    ):
        sems += [dma(shape), dma(shape)]
    conc, loss, grad = pl.pallas_call(
        kernel,
        out_shape=(
            jax.ShapeDtypeStruct((1, CENT), F32),
            jax.ShapeDtypeStruct((1, NP * ROWS), F32),
            jax.ShapeDtypeStruct((NP * ROWS, WIDTH), BF16),
        ),
        in_specs=[pl.BlockSpec(memory_space=pl.ANY)] * 3 + [pl.BlockSpec(memory_space=vmem)] * 2,
        out_specs=(pl.BlockSpec(memory_space=vmem),) * 3,
        scratch_shapes=[
            vmem((NP, CENT, WIDTH), BF16),
            vmem((NX, NZ, ROWS, WIDTH), BF16),
            vmem((NX, NZ, 1, 128), F32),
            vmem((NX - 1, NZ, ROWS, WIDTH), BF16),
            vmem((NZ, NX, ROWS, WIDTH), BF16),
            vmem((NX - 1, NZ, 1, 128), F32),
            vmem((NZ, NX, 1, 128), F32),
            vmem((NP, 1, CENT), F32),
            vmem((NP, QS, CENT), F32),
            vmem((QS, 128), F32),
            vmem((NX, 8, QS), F32),
            vmem((NZ, 8, QS), F32),
            vmem((QS, 128), F32),
            vmem((QS, 128), F32),
            vmem((NX - 1, NZ, ROWS, WIDTH), BF16),
            vmem((NX - 1, NZ, ROWS, WIDTH), BF16),
            vmem((NZ, ROWS, WIDTH), BF16),
            vmem((NZ - 1, ROWS, WIDTH), BF16),
            vmem((NZ * ROWS, WIDTH), F32),
            vmem((NP, ROWS, WIDTH), BF16),
            vmem((NP, ROWS, 128), F32),
            dma((3,)),
            *sems,
        ],
        compiler_params=pltpu.CompilerParams(
            collective_id=0, has_side_effects=True, vmem_limit_bytes=56 * 1024 * 1024
        ),
        name="protonce",
    )(
        centroids,
        queries.reshape(NP, ROWS, WIDTH),
        members.reshape(NZ, NX, NP, ROWS, WIDTH),
        slot,
        pos,
    )
    return conc.reshape(CENT), loss.reshape(NP * ROWS), grad


def solution(mesh):
    placed = (
        P(("dp", "proto"), None),
        P("dp", None),
        P("dp"),
        P("dp", None, None, None, None),
        P("dp", None, None, None),
        P("dp", None, None),
    )
    return jax.shard_map(
        on_device,
        mesh=mesh,
        in_specs=placed,
        out_specs=(P(("dp", "proto")), P("dp"), P("dp", None)),
        check_vma=False,
    )
```

time: 550 us -> 90.7 us (0.16)
  waiting for transfers between devices: 247 us -> 0 us
  blocking collectives: 228 us -> 0 us
  Pallas kernels: 0 us -> 83.1 us
  matrix products: 22.3 us -> 0 us
  starting transfers between devices: 19.6 us -> 0 us
  between operations: 14.2 us -> 0.66 us
  other arithmetic: 8.13 us -> 1.44 us
    reduce_scatter x1 -> x0, waiting for transfers between devices: 230 us -> none  [on_device(): lax.psum_scatter(jnp.dot(weight, centroids, preferred_element_type=jnp.fl...]
    psum x2 -> x0, blocking collectives: 104 us -> none  [the longest x1 74 us: on_device(): row_sum, target = lax.psum((local_sum, target_part), ('dp', 'proto'))]
    pallas_call x0 -> x1, Pallas kernels: none -> 83.1 us  [on_device(): pl.pallas_call(kernel, out_shape=(jax.ShapeDtypeStruct((1, CENT), F32), j...]
    pmax x1 -> x0, blocking collectives: 76.3 us -> none  [on_device(): row_max = lax.pmax(local_max, ('dp', 'proto'))]
    all_gather x1 -> x0, blocking collectives: 48.1 us -> none  [on_device(): lax.all_gather(positive, 'dp', axis=0, tiled=True)]
    dot_general x4 -> x0, matrix products: 22.3 us -> none  [the longest x1 13.1 us: on_device(): jnp.dot(weight, centroids, preferred_element_type=jnp.float32)]
    all_to_all x3 -> x0, starting transfers between devices: 19.6 us -> none  [the longest x1 11.9 us: on_device(): lax.all_to_all(count_mine, 'dp', split_axis=1, concat_axis=0, tiled=True)]
    all_to_all x3 -> x0, waiting for transfers between devices: 13.7 us -> none  [the longest x1 7.16 us: on_device(): lax.all_to_all(count_mine, 'dp', split_axis=1, concat_axis=0, tiled=True)]
  transfers between devices with their start and end apart: 5 -> 0, of which waited for: 4 -> 0; matrix products, arithmetic and copies ran while one was open for 2% -> 0% of each run, Pallas kernels for 0% -> 0%
where the time goes in v1:
time: 90.7 us; the launch traced here: 90.4 us
  Pallas kernels  83.1 us (92%)
  local copies, waits for them, and re-layouts  5.21 us (6%)
  other arithmetic  1.44 us (2%)
    pallas_call x1, Pallas kernels, on_device(): pl.pallas_call(kernel, out_shape=(jax.ShapeDtypeStruct((1, CENT), F32), j...  83.1 us
    unnamed x6, local copies, waits for them, and re-layouts  4.08 us

profile of v1, /device:TPU:1, one launch (start us, length us, event | category | flops | bytes accessed | tf_op | source)
XLA Modules:
  0.0 90.4 jit_solution(6857288965154951663)
XLA Ops:
  0.6 0.0 copy-start
  0.7 0.7 dynamic-slice_convert_fusion
  1.4 0.5 pad_bitcast_fusion.pos
  1.9 0.0 copy-done
  1.9 0.7 fusion
  2.6 0.1 copy.10
  2.7 0.6 pad.8.clone
  3.3 83.1 %protonce.1 = (f32[1,512]{1,0:T(1,128)}, f32[1,128]{1,0:T(1,128)}, bf16[128,768]{1,0:T(8,128)(2,1)}) custom-call(bf16[512,768]{1,0:T(8,128)(2,1)} %cent.1, bf16[8,16,768]{2,1,0:T(8,128)(2,1)} %bitcast.14, bf16[8,4,8,16,768]{4,3,2,1,0:T(8,128)(2,1)} %bitcast.13, f32[8,4,1,128]{3,2,1,0:T(1,128)} %bitcast.15, f32[1,128]{1,0:T(1,128)} %pad_bitcast_fusion.pos), custom_call_target="tpu_custom_call" | custom-call | tf_op jit(solution)/shard_map/protonce/pallas_call | solution.py:325
  86.4 1.2 %copy.14 = f32[512]{0:T(512)} copy(f32[512]{0:T(512)} %bitcast.16) | data formatting | bytes 4096
  87.7 1.1 %copy.15 = f32[128]{0:T(128)} copy(f32[128]{0:T(128)} %bitcast.17) | data formatting | bytes 1024
  88.8 1.6 %copy.16 = bf16[128,768]{1,0:T(8,128)(2,1)} copy(bf16[128,768]{1,0:T(8,128)(2,1)} %get-tuple-element.14) | data formatting | bytes 393216
  (1 shorter events, 0.0 us)
Async XLA Ops:
  0.6 1.3 %copy-start = (s32[1,32,8]{1,2,0:T(8,128)S(1)}, s32[1,32,8]{1,2,0:T(8,128)}, u32[]{:S(2)}) copy-start(s32[1,32,8]{1,2,0:T(8,128)} %param.11) | copy-start | bytes 3076

commit v2 on v1

v2 whole, which is shorter than its diff:
```python
import jax
import jax.numpy as jnp
from jax import lax
from jax.experimental import pallas as pl
from jax.experimental.pallas import tpu as pltpu
from jax.sharding import PartitionSpec as P

MESH = pl.DeviceIdType.MESH
NX, NZ, NP = 4, 8, 8
ROWS, WIDTH, CENT = 16, 768, 512
QS = NX * NZ * ROWS
F32, BF16 = jnp.float32, jnp.bfloat16
LOG2E, LN2 = 1.4426950408889634, 0.6931471805599453


def remote(src, dst, send, recv, device):
    return pltpu.make_async_remote_copy(
        src_ref=src, dst_ref=dst, send_sem=send, recv_sem=recv, device_id=device, device_id_type=MESH
    )


def columns_of(rows):
    n = rows.shape[0]
    wide = jnp.broadcast_to(rows, (n, ROWS, 128))
    lane = lax.broadcasted_iota(jnp.int32, (n, ROWS, 128), 2)
    sub = lax.broadcasted_iota(jnp.int32, (n, ROWS, 128), 1)
    return jnp.sum(jnp.where(lane == sub, wide, 0.0), axis=2, keepdims=True).reshape(n * ROWS, 1)


def kernel(
    cent, qry, mem, slot_in, count_in, pos_in, conc_o, lfin, fin,
    call, qall, pall, mx, mall, slx, sall, invall, score, wgt, peak, sums, sxb, szb, colr, posb, posw,
    gsum, psum, slot, pos, tsend, trx, thz, tsum, gsend, grx, hsend, hz, acc,
    local, mx_s, mx_r, sx_s, sx_r, mz_s, mz_r, sz_s, sz_r, qz_s, qz_r, qx_s, qx_r, pz_s, pz_r, px_s, px_r,
    cy_s, cy_r, cc_s, cc_r, iv_s, iv_r, tx_s, tx_r, tz_s, tz_r, gx_s, gx_r, gz_s, gz_r, fn_s, fn_r, ln_s, ln_r,
    ux_s, ux_r, uz_s, uz_r,
):
    dp = lax.axis_index("dp")
    p = lax.axis_index("proto")
    z, x = dp // NX, dp % NX
    y, c = p // 2, p % 2

    def at_x(d):
        return (x + d) % NX

    def at_z(d):
        return (z + d) % NZ

    def at_p(d):
        return (p + d) % NP

    def dev_x(d):
        return {"dp": z * NX + at_x(d), "proto": p}

    def dev_z(d):
        return {"dp": at_z(d) * NX + x, "proto": p}

    def dev_p(q):
        return {"dp": dp, "proto": q}

    barrier = pltpu.get_barrier_semaphore()
    for d in range(1, NX):
        pl.semaphore_signal(barrier, inc=1, device_id=dev_x(d), device_id_type=MESH)
    for d in range(1, NZ):
        pl.semaphore_signal(barrier, inc=1, device_id=dev_z(d), device_id_type=MESH)
    for d in range(1, NP):
        pl.semaphore_signal(barrier, inc=1, device_id=dev_p(at_p(d)), device_id_type=MESH)

    used = lax.broadcasted_iota(jnp.int32, (ROWS, NX * NZ), 0) < count_in[pl.ds(p, 1), :]
    ids = jnp.where(used, slot_in[p], -1).astype(F32)
    ids = jnp.concatenate([ids, jnp.zeros((ROWS, 128 - NX * NZ), F32)], axis=1)
    ids = jnp.concatenate([ids, jnp.zeros((128 - ROWS, 128), F32)], axis=0).T
    for i in range(NX * NZ):
        slot[i // NX, i % NX] = ids[i : i + 1, :]
    wide = jnp.broadcast_to(pos_in[...].astype(F32), (8, 128))
    pos[...] = pltpu.roll(wide, (128 - p * ROWS) % 128, 1)[0:1, :]

    pl.semaphore_wait(barrier, NX + NZ + NP - 3)

    sends = []

    def go(copy):
        copy.start()
        sends.append(copy)

    z_order = (4, 3, 5, 2, 6, 1, 7)
    half = CENT // 2
    top, bottom = pl.ds(0, half), pl.ds(half, half)
    up = ((y + 1) % 4) * 2 + c
    down = ((y + 3) % 4) * 2 + c
    far = ((y + 2) % 4) * 2 + c
    mate = y * 2 + (1 - c)

    for d in z_order:
        go(remote(pos, pall.at[x, z], pz_s.at[d - 1], pz_r.at[d - 1], dev_z(d)))
    for d in z_order:
        go(remote(qry.at[p], qall.at[x, z], qz_s.at[d - 1], qz_r.at[d - 1], dev_z(d)))
    go(remote(cent.at[top], call.at[p, top], cy_s.at[0], cy_r.at[0], dev_p(up)))
    go(remote(cent.at[bottom], call.at[p, bottom], cy_s.at[3], cy_r.at[3], dev_p(down)))
    go(remote(cent.at[bottom], call.at[p, bottom], cy_s.at[1], cy_r.at[1], dev_p(up)))
    go(remote(cent.at[top], call.at[p, top], cy_s.at[2], cy_r.at[2], dev_p(down)))
    go(remote(cent, call.at[p], cc_s.at[0], cc_r.at[0], dev_p(mate)))
    for d in (2, 1, 3):
        go(remote(mem.at[:, at_x(d), p], mx.at[d - 1], mx_s.at[d - 1], mx_r.at[d - 1], dev_x(d)))
        go(remote(slot.at[:, at_x(d)], slx.at[d - 1], sx_s.at[d - 1], sx_r.at[d - 1], dev_x(d)))
    for d in z_order:
        go(remote(mem.at[at_z(d), x, p], mall.at[z, 0], mz_s.at[0, d - 1], mz_r.at[0, d - 1], dev_z(d)))
        go(remote(slot.at[at_z(d), x], sall.at[z, 0], sz_s.at[0, d - 1], sz_r.at[0, d - 1], dev_z(d)))
    own = (
        pltpu.make_async_copy(cent, call.at[p], local.at[0]),
        pltpu.make_async_copy(qry.at[p], qall.at[x, z], local.at[1]),
        pltpu.make_async_copy(mem.at[z, x, p], mall.at[z, 0], local.at[2]),
    )
    for copy in own:
        copy.start()
    pall[x, z] = pos[...]
    sall[z, 0] = slot[z, x]
    psum[...] = jnp.zeros_like(psum)

    for d in range(1, NZ):
        src = at_z(NZ - d)
        remote(pos, pall.at[x, src], pz_s.at[d - 1], pz_r.at[d - 1], dev_z(d)).wait_recv()
    for d in (2, 1, 3):
        go(remote(pall.at[x], pall.at[x], px_s.at[d - 1], px_r.at[d - 1], dev_x(d)))
    own[1].wait()
    for d in range(1, NZ):
        src = at_z(NZ - d)
        remote(qry.at[p], qall.at[x, src], qz_s.at[d - 1], qz_r.at[d - 1], dev_z(d)).wait_recv()
    for d in (2, 1, 3):
        go(remote(qall.at[x], qall.at[x], qx_s.at[d - 1], qx_r.at[d - 1], dev_x(d)))

    def members_on(d):
        remote(mem.at[:, x, p], mx.at[d - 1], mx_s.at[d - 1], mx_r.at[d - 1], dev_x(d)).wait_recv()
        remote(slot.at[:, x], slx.at[d - 1], sx_s.at[d - 1], sx_r.at[d - 1], dev_x(d)).wait_recv()
        for e in z_order:
            go(remote(mx.at[d - 1, at_z(e)], mall.at[z, d], mz_s.at[d, e - 1], mz_r.at[d, e - 1], dev_z(e)))
            go(remote(slx.at[d - 1, at_z(e)], sall.at[z, d], sz_s.at[d, e - 1], sz_r.at[d, e - 1], dev_z(e)))
        mall[z, d] = mx[d - 1, z]
        sall[z, d] = slx[d - 1, z]

    members_on(1)
    members_on(3)
    remote(cent.at[top], call.at[down, top], cy_s.at[0], cy_r.at[0], dev_p(up)).wait_recv()
    go(remote(call.at[down, top], call.at[down, top], cy_s.at[4], cy_r.at[4], dev_p(up)))
    remote(cent.at[bottom], call.at[up, bottom], cy_s.at[3], cy_r.at[3], dev_p(down)).wait_recv()
    go(remote(call.at[up, bottom], call.at[up, bottom], cy_s.at[5], cy_r.at[5], dev_p(down)))
    go(remote(call.at[down, top], call.at[down, top], cc_s.at[1], cc_r.at[1], dev_p(mate)))
    go(remote(call.at[up, bottom], call.at[up, bottom], cc_s.at[2], cc_r.at[2], dev_p(mate)))
    members_on(2)

    for d in range(1, NX):
        src = at_x(NX - d)
        remote(pall.at[x], pall.at[src], px_s.at[d - 1], px_r.at[d - 1], dev_x(d)).wait_recv()
    base = (dp * (NP * CENT)).astype(F32)
    posb[...] = jnp.broadcast_to(columns_of(pall[...].reshape(NX * NZ, 1, 128)) - base, (QS, 128))

    def positives(chunk):
        here = posb[:, 0:1] - (chunk * CENT).astype(F32)
        hot = lax.broadcasted_iota(jnp.int32, (QS, CENT), 1).astype(F32) == here
        psum[...] += jnp.dot(hot.astype(BF16), call[chunk], preferred_element_type=F32)

    def scores(chunk):
        def rows(i, carry):
            r = pl.ds(i * 2, 2)
            q = qall[r].reshape(2 * NZ * ROWS, WIDTH)
            score[chunk, pl.ds(i * 256, 256), :] = lax.dot_general(
                q, call[chunk], (((1,), (1,)), ((), ())), preferred_element_type=F32
            )
            return carry

        lax.fori_loop(0, 2, rows, 0)

    own[0].wait()
    positives(p)
    remote(cent, call.at[mate], cc_s.at[0], cc_r.at[0], dev_p(mate)).wait_recv()
    positives(mate)
    for d in range(1, NX):
        src = at_x(NX - d)
        remote(qall.at[x], qall.at[src], qx_s.at[d - 1], qx_r.at[d - 1], dev_x(d)).wait_recv()
    scores(p)
    scores(mate)
    remote(cent.at[bottom], call.at[down, bottom], cy_s.at[1], cy_r.at[1], dev_p(up)).wait_recv()
    go(remote(call.at[down, bottom], call.at[down, bottom], cc_s.at[3], cc_r.at[3], dev_p(mate)))
    remote(cent.at[top], call.at[up, top], cy_s.at[2], cy_r.at[2], dev_p(down)).wait_recv()
    go(remote(call.at[up, top], call.at[up, top], cc_s.at[4], cc_r.at[4], dev_p(mate)))
    flip = 1 - 2 * c
    scores(down)
    scores(up)
    remote(call.at[down, top], call.at[down + flip, top], cc_s.at[1], cc_r.at[1], dev_p(mate)).wait_recv()
    remote(call.at[down, bottom], call.at[down + flip, bottom], cc_s.at[3], cc_r.at[3], dev_p(mate)).wait_recv()
    scores(down + flip)
    remote(call.at[up, bottom], call.at[up + flip, bottom], cc_s.at[2], cc_r.at[2], dev_p(mate)).wait_recv()
    remote(call.at[up, top], call.at[up + flip, top], cc_s.at[4], cc_r.at[4], dev_p(mate)).wait_recv()
    scores(up + flip)

    own[2].wait()
    for e in range(1, NZ):
        src = at_z(NZ - e)
        for d in range(NX):
            remote(mem.at[z, x, p], mall.at[src, d], mz_s.at[d, e - 1], mz_r.at[d, e - 1], dev_z(e)).wait_recv()
            remote(slot.at[z, x], sall.at[src, d], sz_s.at[d, e - 1], sz_r.at[d, e - 1], dev_z(e)).wait_recv()
    which = columns_of(sall[...].reshape(NX * NZ, 1, 128))
    cluster = lax.broadcasted_iota(jnp.int32, (QS, CENT), 1).astype(F32)
    hot = which == cluster
    picked = jnp.dot(hot.astype(BF16), call[p], preferred_element_type=F32)
    gap = mall[...].reshape(QS, WIDTH).astype(F32) - picked
    dist = jnp.sqrt(jnp.sum(gap * gap, axis=1, keepdims=True) + 1e-06)
    total = jnp.sum(jnp.where(hot, dist, 0.0), axis=0, keepdims=True)
    count = jnp.sum(hot.astype(F32), axis=0, keepdims=True)
    conc = (total + 1.0) / ((count + 1.0) * jnp.log(count + 10.0))
    conc_o[...] = conc
    invall[p] = 1.0 / conc
    for d in (4, 3, 5, 2, 6, 1, 7):
        go(remote(invall.at[p], invall.at[p], iv_s.at[d - 1], iv_r.at[d - 1], dev_p(at_p(d))))

    positives(down)
    remote(call.at[down, top], call.at[far, top], cy_s.at[4], cy_r.at[4], dev_p(up)).wait_recv()
    go(remote(call.at[far, top], call.at[far, top], cc_s.at[5], cc_r.at[5], dev_p(mate)))
    remote(call.at[up, bottom], call.at[far, bottom], cy_s.at[5], cy_r.at[5], dev_p(down)).wait_recv()
    go(remote(call.at[far, bottom], call.at[far, bottom], cc_s.at[6], cc_r.at[6], dev_p(mate)))
    scores(far)
    remote(call.at[far, top], call.at[far + flip, top], cc_s.at[5], cc_r.at[5], dev_p(mate)).wait_recv()
    remote(call.at[far, bottom], call.at[far + flip, bottom], cc_s.at[6], cc_r.at[6], dev_p(mate)).wait_recv()
    scores(far + flip)
    for d in range(1, NP):
        src = at_p(NP - d)
        remote(invall.at[p], invall.at[src], iv_s.at[d - 1], iv_r.at[d - 1], dev_p(src)).wait_recv()

    step = 16

    def fold(v, op):
        return op(op(v[:, 0:128], v[:, 128:256]), op(v[:, 256:384], v[:, 384:512]))

    def largest(i, carry):
        r = pl.ds(pl.multiple_of(i * step, step), step)
        best = None
        for k in range(NP):
            zed = score[k, r, :] * (invall[k] * LOG2E)
            best = zed if best is None else jnp.maximum(best, zed)
        peak[r, :] = fold(best, jnp.maximum)
        return carry

    lax.fori_loop(0, QS // step, largest, 0)
    peak[...] = jnp.broadcast_to(jnp.max(peak[...], axis=1, keepdims=True), (QS, 128))

    def soft(i, carry):
        r = pl.ds(pl.multiple_of(i * step, step), step)
        most = jnp.concatenate([peak[r, :]] * 4, axis=1)
        added = None
        for k in range(NP):
            e = jnp.exp2(score[k, r, :] * (invall[k] * LOG2E) - most)
            wgt[k, r, :] = (e * invall[k]).astype(BF16)
            added = e if added is None else added + e
        sums[r, :] = fold(added, jnp.add)
        return carry

    lax.fori_loop(0, QS // step, soft, 0)

    lane = lax.broadcasted_iota(jnp.int32, (QS, 128), 1)
    mine = jnp.where(lane == 0, peak[...], jnp.sum(sums[...], axis=1, keepdims=True)).T[0:8, :]
    sxb[x] = mine

    def merged(ref, n):
        best = ref[0][0:1, :]
        for k in range(1, n):
            best = jnp.maximum(best, ref[k][0:1, :])
        added = None
        for k in range(n):
            part = ref[k][1:2, :] * jnp.exp2(ref[k][0:1, :] - best)
            added = part if added is None else added + part
        return best, added

    for d in (2, 1, 3):
        go(remote(sxb.at[x], sxb.at[x], tx_s.at[d - 1], tx_r.at[d - 1], dev_x(d)))

    def weigh(i, carry):
        r = pl.ds(pl.multiple_of(i * 256, 256), 256)
        out = None
        for k in range(NP):
            term = jnp.dot(wgt[k, r, :], call[k], preferred_element_type=F32)
            out = term if out is None else out + term
        gsum[r, :] = out
        return carry

    lax.fori_loop(0, 2, weigh, 0)

    for d in range(1, NX):
        src = at_x(NX - d)
        remote(sxb.at[x], sxb.at[src], tx_s.at[d - 1], tx_r.at[d - 1], dev_x(d)).wait_recv()
    best, added = merged(sxb, NX)
    szb[z] = jnp.concatenate([best, added, jnp.zeros((6, QS), F32)], axis=0)
    for d in z_order:
        go(remote(szb.at[z], szb.at[z], tz_s.at[d - 1], tz_r.at[d - 1], dev_z(d)))

    def hits(i, carry):
        r = pl.ds(pl.multiple_of(i * step, step), step)
        here = jnp.concatenate([posb[r, :]] * 4, axis=1)
        col = lax.broadcasted_iota(jnp.int32, (step, CENT), 1).astype(F32)
        weight, logit = None, None
        for k in range(NP):
            hit = col + float(k * CENT) == here
            a = jnp.where(hit, jnp.broadcast_to(invall[k], (step, CENT)), 0.0)
            b = jnp.where(hit, score[k, r, :], 0.0)
            weight = a if weight is None else weight + a
            logit = b if logit is None else logit + b
        posw[r, :] = fold(weight, jnp.add)
        colr[r, :] = fold(logit, jnp.add)
        return carry

    lax.fori_loop(0, QS // step, hits, 0)
    scale = jnp.sum(posw[...], axis=1, keepdims=True)
    target = jnp.sum(colr[...], axis=1, keepdims=True) * scale
    posw[...] = jnp.broadcast_to(scale, (QS, 128))
    turned = jnp.broadcast_to(target, (QS, 128)).T[0:8, :]
    for b in range(NX):
        tsend[b] = turned[:, b * 128 : (b + 1) * 128]
    positives(up)
    positives(down + flip)
    positives(up + flip)
    positives(far)
    positives(far + flip)

    for d in range(1, NZ):
        src = at_z(NZ - d)
        remote(szb.at[z], szb.at[src], tz_s.at[d - 1], tz_r.at[d - 1], dev_z(d)).wait_recv()
    best, added = merged(szb, NZ)
    share = jnp.exp2(mine[0:1, :] - best) / added
    total_log = best * LN2 + jnp.log(added)
    colr[...] = jnp.concatenate([share, total_log, jnp.zeros((126, QS), F32)], axis=0).T

    def part(block):
        rows = pl.ds(pl.multiple_of(block * (NZ * ROWS), NZ * ROWS), NZ * ROWS)
        return gsum[rows, :] * colr[rows, 0:1] - psum[rows, :] * posw[rows, 0:1]

    for d in (2, 1, 3):
        gsend[d - 1] = part(at_x(d)).astype(BF16).reshape(NZ, ROWS, WIDTH)
        go(remote(gsend.at[d - 1], grx.at[d - 1], gx_s.at[d - 1], gx_r.at[d - 1], dev_x(d)))
        go(remote(tsend.at[at_x(d)], trx.at[d - 1], ux_s.at[d - 1], ux_r.at[d - 1], dev_x(d)))
    acc[...] = part(x)
    told = tsend[x]
    for d in (1, 3, 2):
        remote(tsend.at[x], trx.at[d - 1], ux_s.at[d - 1], ux_r.at[d - 1], dev_x(d)).wait_recv()
        told = told + trx[d - 1]
    tsum[...] = told
    for d in z_order:
        go(remote(tsum, thz.at[d - 1], uz_s.at[d - 1], uz_r.at[d - 1], dev_z(d)))
    for d in (1, 3, 2):
        remote(gsend.at[d - 1], grx.at[d - 1], gx_s.at[d - 1], gx_r.at[d - 1], dev_x(d)).wait_recv()
    summed = acc[...] + (
        grx[0].reshape(NZ * ROWS, WIDTH).astype(F32)
        + grx[1].reshape(NZ * ROWS, WIDTH).astype(F32)
        + grx[2].reshape(NZ * ROWS, WIDTH).astype(F32)
    )
    acc[...] = summed
    hsend[...] = summed.astype(BF16).reshape(NZ, ROWS, WIDTH)
    for d in z_order:
        go(remote(hsend.at[at_z(d)], hz.at[d - 1], gz_s.at[d - 1], gz_r.at[d - 1], dev_z(d)))
    for d in range(1, NZ):
        remote(tsum, thz.at[d - 1], uz_s.at[d - 1], uz_r.at[d - 1], dev_z(d)).wait_recv()
        told = told + thz[d - 1]
    peak[0:128, :] = jnp.concatenate([told, jnp.zeros((120, 128), F32)], axis=0).T
    mine_rows = pl.ds(pl.multiple_of((x * NZ + z) * ROWS, ROWS), ROWS)
    z_rows = pl.ds(pl.multiple_of(z * ROWS, ROWS), ROWS)
    lfin[p] = jnp.broadcast_to(colr[mine_rows, 1:2] - peak[z_rows, 0:1], (ROWS, 128))
    for d in (4, 3, 5, 2, 6, 1, 7):
        go(remote(lfin.at[p], lfin.at[p], ln_s.at[d - 1], ln_r.at[d - 1], dev_p(at_p(d))))
    grad = acc[z_rows, :]
    for d in range(1, NZ):
        remote(hsend.at[z], hz.at[d - 1], gz_s.at[d - 1], gz_r.at[d - 1], dev_z(d)).wait_recv()
        grad = grad + hz[d - 1].astype(F32)

    fin[p] = grad.astype(BF16)
    for d in (4, 3, 5, 2, 6, 1, 7):
        go(remote(fin.at[p], fin.at[p], fn_s.at[d - 1], fn_r.at[d - 1], dev_p(at_p(d))))
    for d in range(1, NP):
        src = at_p(NP - d)
        remote(lfin.at[p], lfin.at[src], ln_s.at[d - 1], ln_r.at[d - 1], dev_p(src)).wait_recv()
        remote(fin.at[p], fin.at[src], fn_s.at[d - 1], fn_r.at[d - 1], dev_p(src)).wait_recv()
    for copy in sends:
        copy.wait_send()


def finish(conc, lfin, fin, conc_o, loss_o, grad_o):
    conc_o[...] = conc[...]
    loss_o[...] = lfin[...].reshape(NP * ROWS, 128).T[0:1, :]
    grad_o[...] = fin[...].reshape(NP * ROWS, WIDTH)


def on_device(centroids, queries, positive, members, member_slot, block_count):
    vmem = pltpu.VMEM
    dma = pltpu.SemaphoreType.DMA
    sems = []
    for shape in (
        (NX - 1,), (NX - 1,), (NX, NZ - 1), (NX, NZ - 1), (NZ - 1,), (NX - 1,), (NZ - 1,), (NX - 1,),
        (6,), (7,), (NP - 1,), (NX - 1,), (NZ - 1,), (NX - 1,), (NZ - 1,), (NP - 1,), (NP - 1,),
        (NX - 1,), (NZ - 1,),
    ):
        sems += [dma(shape), dma(shape)]
    whole = pl.BlockSpec(memory_space=vmem)
    conc, lfin, fin = pl.pallas_call(
        kernel,
        out_shape=(
            jax.ShapeDtypeStruct((1, CENT), F32),
            jax.ShapeDtypeStruct((NP, ROWS, 128), F32),
            jax.ShapeDtypeStruct((NP, ROWS, WIDTH), BF16),
        ),
        in_specs=[pl.BlockSpec(memory_space=pl.ANY)] * 3 + [whole] * 3,
        out_specs=(whole,) * 3,
        scratch_shapes=[
            vmem((NP, CENT, WIDTH), BF16),
            vmem((NX, NZ, ROWS, WIDTH), BF16),
            vmem((NX, NZ, 1, 128), F32),
            vmem((NX - 1, NZ, ROWS, WIDTH), BF16),
            vmem((NZ, NX, ROWS, WIDTH), BF16),
            vmem((NX - 1, NZ, 1, 128), F32),
            vmem((NZ, NX, 1, 128), F32),
            vmem((NP, 1, CENT), F32),
            vmem((NP, QS, CENT), F32),
            vmem((NP, QS, CENT), BF16),
            vmem((QS, 128), F32),
            vmem((QS, 128), F32),
            vmem((NX, 8, QS), F32),
            vmem((NZ, 8, QS), F32),
            vmem((QS, 128), F32),
            vmem((QS, 128), F32),
            vmem((QS, 128), F32),
            vmem((QS, WIDTH), F32),
            vmem((QS, WIDTH), F32),
            vmem((NZ, NX, 1, 128), F32),
            vmem((1, 128), F32),
            vmem((NX, 8, 128), F32),
            vmem((NX - 1, 8, 128), F32),
            vmem((NZ - 1, 8, 128), F32),
            vmem((8, 128), F32),
            vmem((NX - 1, NZ, ROWS, WIDTH), BF16),
            vmem((NX - 1, NZ, ROWS, WIDTH), BF16),
            vmem((NZ, ROWS, WIDTH), BF16),
            vmem((NZ - 1, ROWS, WIDTH), BF16),
            vmem((NZ * ROWS, WIDTH), F32),
            dma((3,)),
            *sems,
        ],
        compiler_params=pltpu.CompilerParams(
            collective_id=0, has_side_effects=True, vmem_limit_bytes=56 * 1024 * 1024
        ),
        name="protonce",
    )(
        centroids,
        queries.reshape(NP, ROWS, WIDTH),
        members.reshape(NZ, NX, NP, ROWS, WIDTH),
        member_slot.transpose(0, 2, 3, 1).reshape(NP, ROWS, NX * NZ),
        block_count.transpose(0, 2, 1).reshape(NP, NX * NZ),
        positive.reshape(1, NP * ROWS),
    )
    conc, loss, grad = pl.pallas_call(
        finish,
        out_shape=(
            jax.ShapeDtypeStruct((1, CENT), F32),
            jax.ShapeDtypeStruct((1, NP * ROWS), F32),
            jax.ShapeDtypeStruct((NP * ROWS, WIDTH), BF16),
        ),
        in_specs=[whole] * 3,
        out_specs=(whole,) * 3,
        name="finish",
    )(conc, lfin, fin)
    return conc.reshape(CENT), loss.reshape(NP * ROWS), grad


def solution(mesh):
    placed = (
        P(("dp", "proto"), None),
        P("dp", None),
        P("dp"),
        P("dp", None, None, None, None),
        P("dp", None, None, None),
        P("dp", None, None),
    )
    return jax.shard_map(
        on_device,
        mesh=mesh,
        in_specs=placed,
        out_specs=(P(("dp", "proto")), P("dp"), P("dp", None)),
        check_vma=False,
    )
```

time: 90.7 us -> 81.4 us (0.90)
  local copies, waits for them, and re-layouts: 5.21 us -> 0 us
  Pallas kernels: 83.1 us -> 80.5 us
  other arithmetic: 1.44 us -> 0 us
    pallas_call x1, Pallas kernels: 83.1 us -> 78.8 us  [on_device(): pl.pallas_call(kernel, out_shape=(jax.ShapeDtypeStruct((1, CENT), F32), j...]
    unnamed x6 -> x0, local copies, waits for them, and re-layouts: 4.08 us -> none
    pallas_call x0 -> x1, Pallas kernels: none -> 1.72 us  [on_device(): pl.pallas_call(finish, out_shape=(jax.ShapeDtypeStruct((1, CENT), F32), j...]
    convert_element_type x2 -> x0, other arithmetic: 1.44 us -> none  [the longest x1 0.73 us: on_device(): pos = lax.dynamic_slice_in_dim(positive, column * ROWS, ROWS).astype(F32)]
where the time goes in v2:
time: 81.4 us; the launch traced here: 81.1 us
  Pallas kernels  80.5 us (99%)
    pallas_call x1, Pallas kernels, on_device(): pl.pallas_call(kernel, out_shape=(jax.ShapeDtypeStruct((1, CENT), F32), j...  78.8 us
    pallas_call x1, Pallas kernels, on_device(): pl.pallas_call(finish, out_shape=(jax.ShapeDtypeStruct((1, CENT), F32), j...  1.72 us

profile of v2, /device:TPU:1, one launch (start us, length us, event | category | flops | bytes accessed | tf_op | source)
XLA Modules:
  0.0 81.1 jit_solution(8879874048417863798)
XLA Ops:
  0.6 78.8 %protonce.1 = (f32[1,512]{1,0:T(1,128)}, f32[8,16,128]{2,1,0:T(8,128)}, bf16[8,16,768]{2,1,0:T(8,128)(2,1)}) custom-call(bf16[512,768]{1,0:T(8,128)(2,1)} %cent.1, bf16[8,16,768]{2,1,0:T(8,128)(2,1)} %bitcast.12, bf16[8,4,8,16,768]{4,3,2,1,0:T(8,128)(2,1)} %bitcast.11, s32[8,16,32]{2,1,0:T(8,128)} %bitcast.13, s32[8,32]{1,0:T(8,128)} %bitcast.14, ...), custom_call_target="tpu_custom_call" | custom-call | tf_op jit(solution)/shard_map/protonce/pallas_call | solution.py:400
  79.4 1.7 %finish.1 = (f32[1,512]{1,0:T(1,128)}, f32[1,128]{1,0:T(1,128)}, bf16[128,768]{1,0:T(8,128)(2,1)}) custom-call(f32[1,512]{1,0:T(1,128)} %get-tuple-element.9.conc, f32[8,16,128]{2,1,0:T(8,128)} %get-tuple-element.10.lfin, bf16[8,16,768]{2,1,0:T(8,128)(2,1)} %get-tuple-element.11.fin), custom_call_target="tpu_custom_call" | custom-call | tf_op jit(solution)/shard_map/finish/pallas_call | solution.py:455

commit v3 on v2

--- a/solution.py
+++ b/solution.py
@@ -9,6 +9,8 @@
 NX, NZ, NP = 4, 8, 8
 ROWS, WIDTH, CENT = 16, 768, 512
 QS = NX * NZ * ROWS
+CA = 512
+CB = WIDTH - CA
 F32, BF16 = jnp.float32, jnp.bfloat16
 LOG2E, LN2 = 1.4426950408889634, 0.6931471805599453
 
@@ -30,10 +32,10 @@
 def kernel(
     cent, qry, mem, slot_in, count_in, pos_in, conc_o, lfin, fin,
     call, qall, pall, mx, mall, slx, sall, invall, score, wgt, peak, sums, sxb, szb, colr, posb, posw,
-    gsum, psum, slot, pos, tsend, trx, thz, tsum, gsend, grx, hsend, hz, acc,
+    gsum, psum, slot, pos, tsend, trx, thz, tsum, ga, gra, ha, hza, acca, gb, grb, hb, hxb, accb,
     local, mx_s, mx_r, sx_s, sx_r, mz_s, mz_r, sz_s, sz_r, qz_s, qz_r, qx_s, qx_r, pz_s, pz_r, px_s, px_r,
     cy_s, cy_r, cc_s, cc_r, iv_s, iv_r, tx_s, tx_r, tz_s, tz_r, gx_s, gx_r, gz_s, gz_r, fn_s, fn_r, ln_s, ln_r,
-    ux_s, ux_r, uz_s, uz_r,
+    ux_s, ux_r, uz_s, uz_r, bz_s, bz_r, bx_s, bx_r,
 ):
     dp = lax.axis_index("dp")
     p = lax.axis_index("proto")
@@ -86,6 +88,9 @@
     z_order = (4, 3, 5, 2, 6, 1, 7)
     half = CENT // 2
     top, bottom = pl.ds(0, half), pl.ds(half, half)
+    cut = 176
+    tops = (pl.ds(0, cut), pl.ds(cut, half - cut))
+    bottoms = (pl.ds(half, cut), pl.ds(half + cut, half - cut))
     up = ((y + 1) % 4) * 2 + c
     down = ((y + 3) % 4) * 2 + c
     far = ((y + 2) % 4) * 2 + c
@@ -100,7 +105,7 @@
     go(remote(cent.at[bottom], call.at[p, bottom], cy_s.at[1], cy_r.at[1], dev_p(up)))
     go(remote(cent.at[top], call.at[p, top], cy_s.at[2], cy_r.at[2], dev_p(down)))
     go(remote(cent, call.at[p], cc_s.at[0], cc_r.at[0], dev_p(mate)))
-    for d in (2, 1, 3):
+    for d in (1, 3, 2):
         go(remote(mem.at[:, at_x(d), p], mx.at[d - 1], mx_s.at[d - 1], mx_r.at[d - 1], dev_x(d)))
         go(remote(slot.at[:, at_x(d)], slx.at[d - 1], sx_s.at[d - 1], sx_r.at[d - 1], dev_x(d)))
     for d in z_order:
@@ -141,9 +146,11 @@
     members_on(1)
     members_on(3)
     remote(cent.at[top], call.at[down, top], cy_s.at[0], cy_r.at[0], dev_p(up)).wait_recv()
-    go(remote(call.at[down, top], call.at[down, top], cy_s.at[4], cy_r.at[4], dev_p(up)))
+    for i, r in enumerate(tops):
+        go(remote(call.at[down, r], call.at[down, r], cy_s.at[4 + i], cy_r.at[4 + i], dev_p(up)))
     remote(cent.at[bottom], call.at[up, bottom], cy_s.at[3], cy_r.at[3], dev_p(down)).wait_recv()
-    go(remote(call.at[up, bottom], call.at[up, bottom], cy_s.at[5], cy_r.at[5], dev_p(down)))
+    for i, r in enumerate(bottoms):
+        go(remote(call.at[up, r], call.at[up, r], cy_s.at[6 + i], cy_r.at[6 + i], dev_p(down)))
     go(remote(call.at[down, top], call.at[down, top], cc_s.at[1], cc_r.at[1], dev_p(mate)))
     go(remote(call.at[up, bottom], call.at[up, bottom], cc_s.at[2], cc_r.at[2], dev_p(mate)))
     members_on(2)
@@ -157,7 +164,7 @@
     def positives(chunk):
         here = posb[:, 0:1] - (chunk * CENT).astype(F32)
         hot = lax.broadcasted_iota(jnp.int32, (QS, CENT), 1).astype(F32) == here
-        psum[...] += jnp.dot(hot.astype(BF16), call[chunk], preferred_element_type=F32)
+        psum[...] += jnp.dot(hot.astype(BF16), call[chunk], preferred_element_type=F32).reshape(psum.shape)
 
     def scores(chunk):
         def rows(i, carry):
@@ -214,13 +221,17 @@
         go(remote(invall.at[p], invall.at[p], iv_s.at[d - 1], iv_r.at[d - 1], dev_p(at_p(d))))
 
     positives(down)
-    remote(call.at[down, top], call.at[far, top], cy_s.at[4], cy_r.at[4], dev_p(up)).wait_recv()
-    go(remote(call.at[far, top], call.at[far, top], cc_s.at[5], cc_r.at[5], dev_p(mate)))
-    remote(call.at[up, bottom], call.at[far, bottom], cy_s.at[5], cy_r.at[5], dev_p(down)).wait_recv()
-    go(remote(call.at[far, bottom], call.at[far, bottom], cc_s.at[6], cc_r.at[6], dev_p(mate)))
+    for i in range(2):
+        r = tops[i]
+        remote(call.at[down, r], call.at[far, r], cy_s.at[4 + i], cy_r.at[4 + i], dev_p(up)).wait_recv()
+        go(remote(call.at[far, r], call.at[far, r], cc_s.at[5 + i], cc_r.at[5 + i], dev_p(mate)))
+        r = bottoms[i]
+        remote(call.at[up, r], call.at[far, r], cy_s.at[6 + i], cy_r.at[6 + i], dev_p(down)).wait_recv()
+        go(remote(call.at[far, r], call.at[far, r], cc_s.at[7 + i], cc_r.at[7 + i], dev_p(mate)))
     scores(far)
-    remote(call.at[far, top], call.at[far + flip, top], cc_s.at[5], cc_r.at[5], dev_p(mate)).wait_recv()
-    remote(call.at[far, bottom], call.at[far + flip, bottom], cc_s.at[6], cc_r.at[6], dev_p(mate)).wait_recv()
+    for i in range(4):
+        r = (tops + bottoms)[i]
+        remote(call.at[far, r], call.at[far + flip, r], cc_s.at[5 + i], cc_r.at[5 + i], dev_p(mate)).wait_recv()
     scores(far + flip)
     for d in range(1, NP):
         src = at_p(NP - d)
@@ -279,7 +290,7 @@
         for k in range(NP):
             term = jnp.dot(wgt[k, r, :], call[k], preferred_element_type=F32)
             out = term if out is None else out + term
-        gsum[r, :] = out
+        gsum[pl.ds(i * 2, 2)] = out.reshape(2, NZ, ROWS, WIDTH)
         return carry
 
     lax.fori_loop(0, 2, weigh, 0)
@@ -303,14 +314,14 @@
             b = jnp.where(hit, score[k, r, :], 0.0)
             weight = a if weight is None else weight + a
             logit = b if logit is None else logit + b
-        posw[r, :] = fold(weight, jnp.add)
-        colr[r, :] = fold(logit, jnp.add)
+        sums[r, :] = fold(weight, jnp.add)
+        peak[r, :] = fold(logit, jnp.add)
         return carry
 
     lax.fori_loop(0, QS // step, hits, 0)
-    scale = jnp.sum(posw[...], axis=1, keepdims=True)
-    target = jnp.sum(colr[...], axis=1, keepdims=True) * scale
-    posw[...] = jnp.broadcast_to(scale, (QS, 128))
+    scale = jnp.sum(sums[...], axis=1, keepdims=True)
+    target = jnp.sum(peak[...], axis=1, keepdims=True) * scale
+    posw[...] = jnp.broadcast_to(scale, (QS, 128)).reshape(posw.shape)
     turned = jnp.broadcast_to(target, (QS, 128)).T[0:8, :]
     for b in range(NX):
         tsend[b] = turned[:, b * 128 : (b + 1) * 128]
@@ -326,52 +337,74 @@
     best, added = merged(szb, NZ)
     share = jnp.exp2(mine[0:1, :] - best) / added
     total_log = best * LN2 + jnp.log(added)
-    colr[...] = jnp.concatenate([share, total_log, jnp.zeros((126, QS), F32)], axis=0).T
-
-    def part(block):
-        rows = pl.ds(pl.multiple_of(block * (NZ * ROWS), NZ * ROWS), NZ * ROWS)
-        return gsum[rows, :] * colr[rows, 0:1] - psum[rows, :] * posw[rows, 0:1]
-
+    colr[...] = jnp.concatenate([share, total_log, jnp.zeros((126, QS), F32)], axis=0).T.reshape(colr.shape)
+
+    ca, cb = pl.ds(0, CA), pl.ds(CA, CB)
+
+    def part(at, cols):
+        return gsum[at + (slice(None), cols)] * colr[at][..., 0:1] - psum[at + (slice(None), cols)] * posw[at][..., 0:1]
+
+    def part_x(b):
+        return part((b, slice(None)), ca)
+
+    def part_z(b):
+        return part((slice(None), b), cb)
+
+    ga[1] = part_x(at_x(2)).astype(BF16)
+    go(remote(ga.at[1], gra.at[1], gx_s.at[1], gx_r.at[1], dev_x(2)))
+    for d in z_order[:3]:
+        gb[d - 1] = part_z(at_z(d)).astype(BF16)
+        go(remote(gb.at[d - 1], grb.at[d - 1], bz_s.at[d - 1], bz_r.at[d - 1], dev_z(d)))
+    for d in (1, 3):
+        ga[d - 1] = part_x(at_x(d)).astype(BF16)
+        go(remote(ga.at[d - 1], gra.at[d - 1], gx_s.at[d - 1], gx_r.at[d - 1], dev_x(d)))
+    for d in z_order[3:]:
+        gb[d - 1] = part_z(at_z(d)).astype(BF16)
+        go(remote(gb.at[d - 1], grb.at[d - 1], bz_s.at[d - 1], bz_r.at[d - 1], dev_z(d)))
     for d in (2, 1, 3):
-        gsend[d - 1] = part(at_x(d)).astype(BF16).reshape(NZ, ROWS, WIDTH)
-        go(remote(gsend.at[d - 1], grx.at[d - 1], gx_s.at[d - 1], gx_r.at[d - 1], dev_x(d)))
         go(remote(tsend.at[at_x(d)], trx.at[d - 1], ux_s.at[d - 1], ux_r.at[d - 1], dev_x(d)))
-    acc[...] = part(x)
+    acca[...] = part_x(x)
+    accb[...] = part_z(z)
     told = tsend[x]
+    for d in (1, 3, 2):
+        remote(ga.at[d - 1], gra.at[d - 1], gx_s.at[d - 1], gx_r.at[d - 1], dev_x(d)).wait_recv()
+        acca[...] += gra[d - 1].astype(F32)
+    ha[...] = acca[...].astype(BF16)
+    for d in z_order:
+        go(remote(ha.at[at_z(d)], hza.at[d - 1], gz_s.at[d - 1], gz_r.at[d - 1], dev_z(d)))
+    for d in range(1, NZ):
+        remote(gb.at[d - 1], grb.at[d - 1], bz_s.at[d - 1], bz_r.at[d - 1], dev_z(d)).wait_recv()
+        accb[...] += grb[d - 1].astype(F32)
+    hb[...] = accb[...].astype(BF16)
+    for d in (2, 1, 3):
+        go(remote(hb.at[at_x(d)], hxb.at[d - 1], bx_s.at[d - 1], bx_r.at[d - 1], dev_x(d)))
     for d in (1, 3, 2):
         remote(tsend.at[x], trx.at[d - 1], ux_s.at[d - 1], ux_r.at[d - 1], dev_x(d)).wait_recv()
         told = told + trx[d - 1]
     tsum[...] = told
     for d in z_order:
         go(remote(tsum, thz.at[d - 1], uz_s.at[d - 1], uz_r.at[d - 1], dev_z(d)))
+    grad_b = accb[x]
     for d in (1, 3, 2):
-        remote(gsend.at[d - 1], grx.at[d - 1], gx_s.at[d - 1], gx_r.at[d - 1], dev_x(d)).wait_recv()
-    summed = acc[...] + (
-        grx[0].reshape(NZ * ROWS, WIDTH).astype(F32)
-        + grx[1].reshape(NZ * ROWS, WIDTH).astype(F32)
-        + grx[2].reshape(NZ * ROWS, WIDTH).astype(F32)
-    )
-    acc[...] = summed
-    hsend[...] = summed.astype(BF16).reshape(NZ, ROWS, WIDTH)
-    for d in z_order:
-        go(remote(hsend.at[at_z(d)], hz.at[d - 1], gz_s.at[d - 1], gz_r.at[d - 1], dev_z(d)))
+        remote(hb.at[x], hxb.at[d - 1], bx_s.at[d - 1], bx_r.at[d - 1], dev_x(d)).wait_recv()
+        grad_b = grad_b + hxb[d - 1].astype(F32)
+    grad_a = acca[z]
+    for d in range(1, NZ):
+        remote(ha.at[z], hza.at[d - 1], gz_s.at[d - 1], gz_r.at[d - 1], dev_z(d)).wait_recv()
+        grad_a = grad_a + hza[d - 1].astype(F32)
+
+    fin[p, :, ca] = grad_a.astype(BF16)
+    fin[p, :, cb] = grad_b.astype(BF16)
+    for d in (4, 3, 5, 2, 6, 1, 7):
+        go(remote(fin.at[p], fin.at[p], fn_s.at[d - 1], fn_r.at[d - 1], dev_p(at_p(d))))
     for d in range(1, NZ):
         remote(tsum, thz.at[d - 1], uz_s.at[d - 1], uz_r.at[d - 1], dev_z(d)).wait_recv()
         told = told + thz[d - 1]
     peak[0:128, :] = jnp.concatenate([told, jnp.zeros((120, 128), F32)], axis=0).T
-    mine_rows = pl.ds(pl.multiple_of((x * NZ + z) * ROWS, ROWS), ROWS)
     z_rows = pl.ds(pl.multiple_of(z * ROWS, ROWS), ROWS)
-    lfin[p] = jnp.broadcast_to(colr[mine_rows, 1:2] - peak[z_rows, 0:1], (ROWS, 128))
+    lfin[p] = jnp.broadcast_to(colr[x, z][:, 1:2] - peak[z_rows, 0:1], (ROWS, 128))
     for d in (4, 3, 5, 2, 6, 1, 7):
         go(remote(lfin.at[p], lfin.at[p], ln_s.at[d - 1], ln_r.at[d - 1], dev_p(at_p(d))))
-    grad = acc[z_rows, :]
-    for d in range(1, NZ):
-        remote(hsend.at[z], hz.at[d - 1], gz_s.at[d - 1], gz_r.at[d - 1], dev_z(d)).wait_recv()
-        grad = grad + hz[d - 1].astype(F32)
-
-    fin[p] = grad.astype(BF16)
-    for d in (4, 3, 5, 2, 6, 1, 7):
-        go(remote(fin.at[p], fin.at[p], fn_s.at[d - 1], fn_r.at[d - 1], dev_p(at_p(d))))
     for d in range(1, NP):
         src = at_p(NP - d)
         remote(lfin.at[p], lfin.at[src], ln_s.at[d - 1], ln_r.at[d - 1], dev_p(src)).wait_recv()
@@ -392,8 +425,8 @@
     sems = []
     for shape in (
         (NX - 1,), (NX - 1,), (NX, NZ - 1), (NX, NZ - 1), (NZ - 1,), (NX - 1,), (NZ - 1,), (NX - 1,),
-        (6,), (7,), (NP - 1,), (NX - 1,), (NZ - 1,), (NX - 1,), (NZ - 1,), (NP - 1,), (NP - 1,),
-        (NX - 1,), (NZ - 1,),
+        (8,), (9,), (NP - 1,), (NX - 1,), (NZ - 1,), (NX - 1,), (NZ - 1,), (NP - 1,), (NP - 1,),
+        (NX - 1,), (NZ - 1,), (NZ - 1,), (NX - 1,),
     ):
         sems += [dma(shape), dma(shape)]
     whole = pl.BlockSpec(memory_space=vmem)
@@ -421,22 +454,27 @@
             vmem((QS, 128), F32),
             vmem((NX, 8, QS), F32),
             vmem((NZ, 8, QS), F32),
+            vmem((NX, NZ, ROWS, 128), F32),
             vmem((QS, 128), F32),
-            vmem((QS, 128), F32),
-            vmem((QS, 128), F32),
-            vmem((QS, WIDTH), F32),
-            vmem((QS, WIDTH), F32),
+            vmem((NX, NZ, ROWS, 128), F32),
+            vmem((NX, NZ, ROWS, WIDTH), F32),
+            vmem((NX, NZ, ROWS, WIDTH), F32),
             vmem((NZ, NX, 1, 128), F32),
             vmem((1, 128), F32),
             vmem((NX, 8, 128), F32),
             vmem((NX - 1, 8, 128), F32),
             vmem((NZ - 1, 8, 128), F32),
             vmem((8, 128), F32),
-            vmem((NX - 1, NZ, ROWS, WIDTH), BF16),
-            vmem((NX - 1, NZ, ROWS, WIDTH), BF16),
-            vmem((NZ, ROWS, WIDTH), BF16),
-            vmem((NZ - 1, ROWS, WIDTH), BF16),
-            vmem((NZ * ROWS, WIDTH), F32),
+            vmem((NX - 1, NZ, ROWS, CA), BF16),
+            vmem((NX - 1, NZ, ROWS, CA), BF16),
+            vmem((NZ, ROWS, CA), BF16),
+            vmem((NZ - 1, ROWS, CA), BF16),
+            vmem((NZ, ROWS, CA), F32),
+            vmem((NZ - 1, NX, ROWS, CB), BF16),
+            vmem((NZ - 1, NX, ROWS, CB), BF16),
+            vmem((NX, ROWS, CB), BF16),
+            vmem((NX - 1, ROWS, CB), BF16),
+            vmem((NX, ROWS, CB), F32),
             dma((3,)),
             *sems,
         ],

time: 81.4 us -> 78.6 us (0.966)
  Pallas kernels: 80.5 us -> 77.9 us
    pallas_call x1, Pallas kernels: 78.8 us -> 76.1 us  [on_device(): pl.pallas_call(kernel, out_shape=(jax.ShapeDtypeStruct((1, CENT), F32), j...]
where the time goes in v3:
time: 78.6 us; the launch traced here: 78.5 us
  Pallas kernels  77.9 us (99%)
    pallas_call x1, Pallas kernels, on_device(): pl.pallas_call(kernel, out_shape=(jax.ShapeDtypeStruct((1, CENT), F32), j...  76.1 us
    pallas_call x1, Pallas kernels, on_device(): pl.pallas_call(finish, out_shape=(jax.ShapeDtypeStruct((1, CENT), F32), j...  1.72 us

profile of v3, /device:TPU:1, one launch (start us, length us, event | category | flops | bytes accessed | tf_op | source)
XLA Modules:
  0.0 78.5 jit_solution(5105570429567166645)
XLA Ops:
  0.6 76.1 %protonce.1 = (f32[1,512]{1,0:T(1,128)}, f32[8,16,128]{2,1,0:T(8,128)}, bf16[8,16,768]{2,1,0:T(8,128)(2,1)}) custom-call(bf16[512,768]{1,0:T(8,128)(2,1)} %cent.1, bf16[8,16,768]{2,1,0:T(8,128)(2,1)} %bitcast.12, bf16[8,4,8,16,768]{4,3,2,1,0:T(8,128)(2,1)} %bitcast.11, s32[8,16,32]{2,1,0:T(8,128)} %bitcast.13, s32[8,32]{1,0:T(8,128)} %bitcast.14, ...), custom_call_target="tpu_custom_call" | custom-call | tf_op jit(solution)/shard_map/protonce/pallas_call | solution.py:433
  76.8 1.7 %finish.1 = (f32[1,512]{1,0:T(1,128)}, f32[1,128]{1,0:T(1,128)}, bf16[128,768]{1,0:T(8,128)(2,1)}) custom-call(f32[1,512]{1,0:T(1,128)} %get-tuple-element.9.conc, f32[8,16,128]{2,1,0:T(8,128)} %get-tuple-element.10.lfin, bf16[8,16,768]{2,1,0:T(8,128)(2,1)} %get-tuple-element.11.fin), custom_call_target="tpu_custom_call" | custom-call | tf_op jit(solution)/shard_map/finish/pallas_call | solution.py:493

commit v4 on v3

--- a/solution.py
+++ b/solution.py
@@ -31,10 +31,10 @@
 
 def kernel(
     cent, qry, mem, slot_in, count_in, pos_in, conc_o, lfin, fin,
-    call, qall, pall, mx, mall, slx, sall, invall, score, wgt, peak, sums, sxb, szb, colr, posb, posw,
+    call, qall, pall, mx, mall, slx, sall, invall, score, wgt, peak, sums, peakb, sumsb, tile, colr, posb, posw,
     gsum, psum, slot, pos, tsend, trx, thz, tsum, ga, gra, ha, hza, acca, gb, grb, hb, hxb, accb,
     local, mx_s, mx_r, sx_s, sx_r, mz_s, mz_r, sz_s, sz_r, qz_s, qz_r, qx_s, qx_r, pz_s, pz_r, px_s, px_r,
-    cy_s, cy_r, cc_s, cc_r, iv_s, iv_r, tx_s, tx_r, tz_s, tz_r, gx_s, gx_r, gz_s, gz_r, fn_s, fn_r, ln_s, ln_r,
+    cy_s, cy_r, cc_s, cc_r, iv_s, iv_r, st_s, st_r, gx_s, gx_r, gz_s, gz_r, fn_s, fn_r, ln_s, ln_r,
     ux_s, ux_r, uz_s, uz_r, bz_s, bz_r, bx_s, bx_r,
 ):
     dp = lax.axis_index("dp")
@@ -57,14 +57,18 @@
     def dev_z(d):
         return {"dp": at_z(d) * NX + x, "proto": p}
 
+    def dev_xz(d, e):
+        return {"dp": at_z(e) * NX + at_x(d), "proto": p}
+
     def dev_p(q):
         return {"dp": dp, "proto": q}
 
     barrier = pltpu.get_barrier_semaphore()
-    for d in range(1, NX):
-        pl.semaphore_signal(barrier, inc=1, device_id=dev_x(d), device_id_type=MESH)
-    for d in range(1, NZ):
-        pl.semaphore_signal(barrier, inc=1, device_id=dev_z(d), device_id_type=MESH)
+    both = sorted(
+        ((d, e) for d in range(NX) for e in range(NZ) if d + e), key=lambda v: -min(v[0], NX - v[0]) - min(v[1], NZ - v[1])
+    )
+    for d, e in both:
+        pl.semaphore_signal(barrier, inc=1, device_id=dev_xz(d, e), device_id_type=MESH)
     for d in range(1, NP):
         pl.semaphore_signal(barrier, inc=1, device_id=dev_p(at_p(d)), device_id_type=MESH)
 
@@ -77,7 +81,7 @@
     wide = jnp.broadcast_to(pos_in[...].astype(F32), (8, 128))
     pos[...] = pltpu.roll(wide, (128 - p * ROWS) % 128, 1)[0:1, :]
 
-    pl.semaphore_wait(barrier, NX + NZ + NP - 3)
+    pl.semaphore_wait(barrier, NX * NZ + NP - 2)
 
     sends = []
 
@@ -221,6 +225,9 @@
         go(remote(invall.at[p], invall.at[p], iv_s.at[d - 1], iv_r.at[d - 1], dev_p(at_p(d))))
 
     positives(down)
+    positives(up)
+    positives(down + flip)
+    positives(up + flip)
     for i in range(2):
         r = tops[i]
         remote(call.at[down, r], call.at[far, r], cy_s.at[4 + i], cy_r.at[4 + i], dev_p(up)).wait_recv()
@@ -229,79 +236,73 @@
         remote(call.at[up, r], call.at[far, r], cy_s.at[6 + i], cy_r.at[6 + i], dev_p(down)).wait_recv()
         go(remote(call.at[far, r], call.at[far, r], cc_s.at[7 + i], cc_r.at[7 + i], dev_p(mate)))
     scores(far)
+    positives(far)
+    for d in range(1, NP):
+        src = at_p(NP - d)
+        remote(invall.at[p], invall.at[src], iv_s.at[d - 1], iv_r.at[d - 1], dev_p(src)).wait_recv()
+
+    step = 16
+
+    def fold(v, op):
+        return op(op(v[:, 0:128], v[:, 128:256]), op(v[:, 256:384], v[:, 384:512]))
+
+    def soften(chunks, peak, sums):
+        def largest(i, carry):
+            r = pl.ds(pl.multiple_of(i * step, step), step)
+            best = None
+            for k in chunks:
+                zed = score[k, r, :] * (invall[k] * LOG2E)
+                best = zed if best is None else jnp.maximum(best, zed)
+            peak[r, :] = fold(best, jnp.maximum)
+            return carry
+
+        lax.fori_loop(0, QS // step, largest, 0)
+        peak[...] = jnp.broadcast_to(jnp.max(peak[...], axis=1, keepdims=True), (QS, 128))
+
+        def soft(i, carry):
+            r = pl.ds(pl.multiple_of(i * step, step), step)
+            most = jnp.concatenate([peak[r, :]] * 4, axis=1)
+            added = None
+            for k in chunks:
+                e = jnp.exp2(score[k, r, :] * (invall[k] * LOG2E) - most)
+                wgt[k, r, :] = (e * invall[k]).astype(BF16)
+                added = e if added is None else added + e
+            sums[r, :] = fold(added, jnp.add)
+            return carry
+
+        lax.fori_loop(0, QS // step, soft, 0)
+
+    early = (p, mate, down, up, down + flip, up + flip, far)
+    last = far + flip
+    soften(early, peak, sums)
     for i in range(4):
         r = (tops + bottoms)[i]
         remote(call.at[far, r], call.at[far + flip, r], cc_s.at[5 + i], cc_r.at[5 + i], dev_p(mate)).wait_recv()
-    scores(far + flip)
-    for d in range(1, NP):
-        src = at_p(NP - d)
-        remote(invall.at[p], invall.at[src], iv_s.at[d - 1], iv_r.at[d - 1], dev_p(src)).wait_recv()
-
-    step = 16
-
-    def fold(v, op):
-        return op(op(v[:, 0:128], v[:, 128:256]), op(v[:, 256:384], v[:, 384:512]))
-
-    def largest(i, carry):
-        r = pl.ds(pl.multiple_of(i * step, step), step)
-        best = None
-        for k in range(NP):
-            zed = score[k, r, :] * (invall[k] * LOG2E)
-            best = zed if best is None else jnp.maximum(best, zed)
-        peak[r, :] = fold(best, jnp.maximum)
-        return carry
-
-    lax.fori_loop(0, QS // step, largest, 0)
-    peak[...] = jnp.broadcast_to(jnp.max(peak[...], axis=1, keepdims=True), (QS, 128))
-
-    def soft(i, carry):
-        r = pl.ds(pl.multiple_of(i * step, step), step)
-        most = jnp.concatenate([peak[r, :]] * 4, axis=1)
-        added = None
-        for k in range(NP):
-            e = jnp.exp2(score[k, r, :] * (invall[k] * LOG2E) - most)
-            wgt[k, r, :] = (e * invall[k]).astype(BF16)
-            added = e if added is None else added + e
-        sums[r, :] = fold(added, jnp.add)
-        return carry
-
-    lax.fori_loop(0, QS // step, soft, 0)
+    scores(last)
+    soften((last,), peakb, sumsb)
 
     lane = lax.broadcasted_iota(jnp.int32, (QS, 128), 1)
-    mine = jnp.where(lane == 0, peak[...], jnp.sum(sums[...], axis=1, keepdims=True)).T[0:8, :]
-    sxb[x] = mine
-
-    def merged(ref, n):
-        best = ref[0][0:1, :]
-        for k in range(1, n):
-            best = jnp.maximum(best, ref[k][0:1, :])
-        added = None
-        for k in range(n):
-            part = ref[k][1:2, :] * jnp.exp2(ref[k][0:1, :] - best)
-            added = part if added is None else added + part
-        return best, added
-
-    for d in (2, 1, 3):
-        go(remote(sxb.at[x], sxb.at[x], tx_s.at[d - 1], tx_r.at[d - 1], dev_x(d)))
+    most = jnp.maximum(peak[...], peakb[...])
+    peak[...] = jnp.exp2(peak[...] - most)
+    peakb[...] = jnp.exp2(peakb[...] - most)
+    summed = jnp.sum(sums[...] * peak[...] + sumsb[...] * peakb[...], axis=1, keepdims=True)
+    mine = jnp.where(lane == 0, most, summed).T
+    tile[x, z] = jnp.concatenate([mine[i : i + 1, b * 128 : (b + 1) * 128] for i in range(2) for b in range(NX)], axis=0)
+    for d, e in both:
+        go(remote(tile.at[x, z], tile.at[x, z], st_s.at[d * NZ + e], st_r.at[d * NZ + e], dev_xz(d, e)))
 
     def weigh(i, carry):
         r = pl.ds(pl.multiple_of(i * 256, 256), 256)
         out = None
-        for k in range(NP):
+        for k in early:
             term = jnp.dot(wgt[k, r, :], call[k], preferred_element_type=F32)
             out = term if out is None else out + term
+        late = jnp.dot(wgt[last, r, :], call[last], preferred_element_type=F32)
+        out = out * peak[r, 0:1] + late * peakb[r, 0:1]
         gsum[pl.ds(i * 2, 2)] = out.reshape(2, NZ, ROWS, WIDTH)
         return carry
 
     lax.fori_loop(0, 2, weigh, 0)
-
-    for d in range(1, NX):
-        src = at_x(NX - d)
-        remote(sxb.at[x], sxb.at[src], tx_s.at[d - 1], tx_r.at[d - 1], dev_x(d)).wait_recv()
-    best, added = merged(sxb, NX)
-    szb[z] = jnp.concatenate([best, added, jnp.zeros((6, QS), F32)], axis=0)
-    for d in z_order:
-        go(remote(szb.at[z], szb.at[z], tz_s.at[d - 1], tz_r.at[d - 1], dev_z(d)))
 
     def hits(i, carry):
         r = pl.ds(pl.multiple_of(i * step, step), step)
@@ -325,18 +326,20 @@
     turned = jnp.broadcast_to(target, (QS, 128)).T[0:8, :]
     for b in range(NX):
         tsend[b] = turned[:, b * 128 : (b + 1) * 128]
-    positives(up)
-    positives(down + flip)
-    positives(up + flip)
-    positives(far)
-    positives(far + flip)
-
-    for d in range(1, NZ):
-        src = at_z(NZ - d)
-        remote(szb.at[z], szb.at[src], tz_s.at[d - 1], tz_r.at[d - 1], dev_z(d)).wait_recv()
-    best, added = merged(szb, NZ)
-    share = jnp.exp2(mine[0:1, :] - best) / added
-    total_log = best * LN2 + jnp.log(added)
+    positives(last)
+
+    for d, e in both:
+        src = (at_x(NX - d), at_z(NZ - e))
+        remote(tile.at[x, z], tile.at[src], st_s.at[d * NZ + e], st_r.at[d * NZ + e], dev_xz(d, e)).wait_recv()
+    tiles = tile[...].reshape(NX * NZ, 8, 128)
+    best = jnp.max(tiles[:, 0:NX], axis=0)
+    added = jnp.sum(tiles[:, NX:8] * jnp.exp2(tiles[:, 0:NX] - best[None]), axis=0)
+
+    def flat(v):
+        return jnp.concatenate([v[b : b + 1, :] for b in range(NX)], axis=1)
+
+    share = flat(jnp.exp2(tile[x, z][0:NX] - best) / added)
+    total_log = flat(best * LN2 + jnp.log(added))
     colr[...] = jnp.concatenate([share, total_log, jnp.zeros((126, QS), F32)], axis=0).T.reshape(colr.shape)
 
     ca, cb = pl.ds(0, CA), pl.ds(CA, CB)
@@ -425,7 +428,7 @@
     sems = []
     for shape in (
         (NX - 1,), (NX - 1,), (NX, NZ - 1), (NX, NZ - 1), (NZ - 1,), (NX - 1,), (NZ - 1,), (NX - 1,),
-        (8,), (9,), (NP - 1,), (NX - 1,), (NZ - 1,), (NX - 1,), (NZ - 1,), (NP - 1,), (NP - 1,),
+        (8,), (9,), (NP - 1,), (NX * NZ,), (NX - 1,), (NZ - 1,), (NP - 1,), (NP - 1,),
         (NX - 1,), (NZ - 1,), (NZ - 1,), (NX - 1,),
     ):
         sems += [dma(shape), dma(shape)]
@@ -452,8 +455,9 @@
             vmem((NP, QS, CENT), BF16),
             vmem((QS, 128), F32),
             vmem((QS, 128), F32),
-            vmem((NX, 8, QS), F32),
-            vmem((NZ, 8, QS), F32),
+            vmem((QS, 128), F32),
+            vmem((QS, 128), F32),
+            vmem((NX, NZ, 8, 128), F32),
             vmem((NX, NZ, ROWS, 128), F32),
             vmem((QS, 128), F32),
             vmem((NX, NZ, ROWS, 128), F32),

time: 78.6 us -> 79.3 us (level)
  no operation moved by 1% of the time
where the time goes in v4:
time: 79.3 us; the launch traced here: 79.1 us
  Pallas kernels  78.5 us (99%)
    pallas_call x1, Pallas kernels, on_device(): pl.pallas_call(kernel, out_shape=(jax.ShapeDtypeStruct((1, CENT), F32), j...  76.8 us
    pallas_call x1, Pallas kernels, on_device(): pl.pallas_call(finish, out_shape=(jax.ShapeDtypeStruct((1, CENT), F32), j...  1.72 us

profile of v4, /device:TPU:1, one launch (start us, length us, event | category | flops | bytes accessed | tf_op | source)
XLA Modules:
  0.0 79.1 jit_solution(1144485487353488763)
XLA Ops:
  0.6 76.8 %protonce.1 = (f32[1,512]{1,0:T(1,128)}, f32[8,16,128]{2,1,0:T(8,128)}, bf16[8,16,768]{2,1,0:T(8,128)(2,1)}) custom-call(bf16[512,768]{1,0:T(8,128)(2,1)} %cent.1, bf16[8,16,768]{2,1,0:T(8,128)(2,1)} %bitcast.12, bf16[8,4,8,16,768]{4,3,2,1,0:T(8,128)(2,1)} %bitcast.11, s32[8,16,32]{2,1,0:T(8,128)} %bitcast.13, s32[8,32]{1,0:T(8,128)} %bitcast.14, ...), custom_call_target="tpu_custom_call" | custom-call | tf_op jit(solution)/shard_map/protonce/pallas_call | solution.py:436
  77.4 1.7 %finish.1 = (f32[1,512]{1,0:T(1,128)}, f32[1,128]{1,0:T(1,128)}, bf16[128,768]{1,0:T(8,128)(2,1)}) custom-call(f32[1,512]{1,0:T(1,128)} %get-tuple-element.9.conc, f32[8,16,128]{2,1,0:T(8,128)} %get-tuple-element.10.lfin, bf16[8,16,768]{2,1,0:T(8,128)(2,1)} %get-tuple-element.11.fin), custom_call_target="tpu_custom_call" | custom-call | tf_op jit(solution)/shard_map/finish/pallas_call | solution.py:497

commit v5 on v4

--- a/solution.py
+++ b/solution.py
@@ -31,7 +31,7 @@
 
 def kernel(
     cent, qry, mem, slot_in, count_in, pos_in, conc_o, lfin, fin,
-    call, qall, pall, mx, mall, slx, sall, invall, score, wgt, peak, sums, peakb, sumsb, tile, colr, posb, posw,
+    call, qall, pall, mx, mall, slx, sall, invall, score, wgt, peak, sums, peakb, sumsb, hitw, hitz, tile, colr, posb, posw,
     gsum, psum, slot, pos, tsend, trx, thz, tsum, ga, gra, ha, hza, acca, gb, grb, hb, hxb, accb,
     local, mx_s, mx_r, sx_s, sx_r, mz_s, mz_r, sz_s, sz_r, qz_s, qz_r, qx_s, qx_r, pz_s, pz_r, px_s, px_r,
     cy_s, cy_r, cc_s, cc_r, iv_s, iv_r, st_s, st_r, gx_s, gx_r, gz_s, gz_r, fn_s, fn_r, ln_s, ln_r,
@@ -67,10 +67,16 @@
     both = sorted(
         ((d, e) for d in range(NX) for e in range(NZ) if d + e), key=lambda v: -min(v[0], NX - v[0]) - min(v[1], NZ - v[1])
     )
-    for d, e in both:
-        pl.semaphore_signal(barrier, inc=1, device_id=dev_xz(d, e), device_id_type=MESH)
-    for d in range(1, NP):
-        pl.semaphore_signal(barrier, inc=1, device_id=dev_p(at_p(d)), device_id_type=MESH)
+    up = ((y + 1) % 4) * 2 + c
+    down = ((y + 3) % 4) * 2 + c
+    far = ((y + 2) % 4) * 2 + c
+    mate = y * 2 + (1 - c)
+    for d in (4, 3, 5, 2, 6, 1, 7):
+        pl.semaphore_signal(barrier, inc=1, device_id=dev_z(d), device_id_type=MESH)
+    for d in (2, 1, 3):
+        pl.semaphore_signal(barrier, inc=1, device_id=dev_x(d), device_id_type=MESH)
+    for q in (up, down, mate):
+        pl.semaphore_signal(barrier, inc=1, device_id=dev_p(q), device_id_type=MESH)
 
     used = lax.broadcasted_iota(jnp.int32, (ROWS, NX * NZ), 0) < count_in[pl.ds(p, 1), :]
     ids = jnp.where(used, slot_in[p], -1).astype(F32)
@@ -81,7 +87,7 @@
     wide = jnp.broadcast_to(pos_in[...].astype(F32), (8, 128))
     pos[...] = pltpu.roll(wide, (128 - p * ROWS) % 128, 1)[0:1, :]
 
-    pl.semaphore_wait(barrier, NX * NZ + NP - 2)
+    pl.semaphore_wait(barrier, NX + NZ + 1)
 
     sends = []
 
@@ -95,10 +101,6 @@
     cut = 176
     tops = (pl.ds(0, cut), pl.ds(cut, half - cut))
     bottoms = (pl.ds(half, cut), pl.ds(half + cut, half - cut))
-    up = ((y + 1) % 4) * 2 + c
-    down = ((y + 3) % 4) * 2 + c
-    far = ((y + 2) % 4) * 2 + c
-    mate = y * 2 + (1 - c)
 
     for d in z_order:
         go(remote(pos, pall.at[x, z], pz_s.at[d - 1], pz_r.at[d - 1], dev_z(d)))
@@ -236,7 +238,6 @@
         remote(call.at[up, r], call.at[far, r], cy_s.at[6 + i], cy_r.at[6 + i], dev_p(down)).wait_recv()
         go(remote(call.at[far, r], call.at[far, r], cc_s.at[7 + i], cc_r.at[7 + i], dev_p(mate)))
     scores(far)
-    positives(far)
     for d in range(1, NP):
         src = at_p(NP - d)
         remote(invall.at[p], invall.at[src], iv_s.at[d - 1], iv_r.at[d - 1], dev_p(src)).wait_recv()
@@ -298,34 +299,33 @@
             term = jnp.dot(wgt[k, r, :], call[k], preferred_element_type=F32)
             out = term if out is None else out + term
         late = jnp.dot(wgt[last, r, :], call[last], preferred_element_type=F32)
+        for s in range(0, 256, step):
+            q = pl.ds(pl.multiple_of(i * 256 + s, step), step)
+            here = jnp.concatenate([posb[q, :]] * 4, axis=1)
+            col = lax.broadcasted_iota(jnp.int32, (step, CENT), 1).astype(F32)
+            weight, logit = None, None
+            for k in range(NP):
+                hit = col == here - float(k * CENT)
+                a = jnp.where(hit, jnp.broadcast_to(invall[k], (step, CENT)), 0.0)
+                b = jnp.where(hit, score[k, q, :], 0.0)
+                weight = a if weight is None else weight + a
+                logit = b if logit is None else logit + b
+            hitw[q, :] = fold(weight, jnp.add)
+            hitz[q, :] = fold(logit, jnp.add)
         out = out * peak[r, 0:1] + late * peakb[r, 0:1]
         gsum[pl.ds(i * 2, 2)] = out.reshape(2, NZ, ROWS, WIDTH)
         return carry
 
     lax.fori_loop(0, 2, weigh, 0)
-
-    def hits(i, carry):
-        r = pl.ds(pl.multiple_of(i * step, step), step)
-        here = jnp.concatenate([posb[r, :]] * 4, axis=1)
-        col = lax.broadcasted_iota(jnp.int32, (step, CENT), 1).astype(F32)
-        weight, logit = None, None
-        for k in range(NP):
-            hit = col + float(k * CENT) == here
-            a = jnp.where(hit, jnp.broadcast_to(invall[k], (step, CENT)), 0.0)
-            b = jnp.where(hit, score[k, r, :], 0.0)
-            weight = a if weight is None else weight + a
-            logit = b if logit is None else logit + b
-        sums[r, :] = fold(weight, jnp.add)
-        peak[r, :] = fold(logit, jnp.add)
-        return carry
-
-    lax.fori_loop(0, QS // step, hits, 0)
-    scale = jnp.sum(sums[...], axis=1, keepdims=True)
-    target = jnp.sum(peak[...], axis=1, keepdims=True) * scale
+    scale = jnp.sum(hitw[...], axis=1, keepdims=True)
+    target = jnp.sum(hitz[...], axis=1, keepdims=True) * scale
     posw[...] = jnp.broadcast_to(scale, (QS, 128)).reshape(posw.shape)
     turned = jnp.broadcast_to(target, (QS, 128)).T[0:8, :]
     for b in range(NX):
         tsend[b] = turned[:, b * 128 : (b + 1) * 128]
+    for d in (2, 1, 3):
+        go(remote(tsend.at[at_x(d)], trx.at[d - 1], ux_s.at[d - 1], ux_r.at[d - 1], dev_x(d)))
+    positives(far)
     positives(last)
 
     for d, e in both:
@@ -364,11 +364,15 @@
     for d in z_order[3:]:
         gb[d - 1] = part_z(at_z(d)).astype(BF16)
         go(remote(gb.at[d - 1], grb.at[d - 1], bz_s.at[d - 1], bz_r.at[d - 1], dev_z(d)))
-    for d in (2, 1, 3):
-        go(remote(tsend.at[at_x(d)], trx.at[d - 1], ux_s.at[d - 1], ux_r.at[d - 1], dev_x(d)))
+    told = tsend[x]
+    for d in (1, 3, 2):
+        remote(tsend.at[x], trx.at[d - 1], ux_s.at[d - 1], ux_r.at[d - 1], dev_x(d)).wait_recv()
+        told = told + trx[d - 1]
+    tsum[...] = told
+    for d in z_order:
+        go(remote(tsum, thz.at[d - 1], uz_s.at[d - 1], uz_r.at[d - 1], dev_z(d)))
     acca[...] = part_x(x)
     accb[...] = part_z(z)
-    told = tsend[x]
     for d in (1, 3, 2):
         remote(ga.at[d - 1], gra.at[d - 1], gx_s.at[d - 1], gx_r.at[d - 1], dev_x(d)).wait_recv()
         acca[...] += gra[d - 1].astype(F32)
@@ -381,12 +385,14 @@
     hb[...] = accb[...].astype(BF16)
     for d in (2, 1, 3):
         go(remote(hb.at[at_x(d)], hxb.at[d - 1], bx_s.at[d - 1], bx_r.at[d - 1], dev_x(d)))
-    for d in (1, 3, 2):
-        remote(tsend.at[x], trx.at[d - 1], ux_s.at[d - 1], ux_r.at[d - 1], dev_x(d)).wait_recv()
-        told = told + trx[d - 1]
-    tsum[...] = told
-    for d in z_order:
-        go(remote(tsum, thz.at[d - 1], uz_s.at[d - 1], uz_r.at[d - 1], dev_z(d)))
+    for d in range(1, NZ):
+        remote(tsum, thz.at[d - 1], uz_s.at[d - 1], uz_r.at[d - 1], dev_z(d)).wait_recv()
+        told = told + thz[d - 1]
+    peak[0:128, :] = jnp.concatenate([told, jnp.zeros((120, 128), F32)], axis=0).T
+    z_rows = pl.ds(pl.multiple_of(z * ROWS, ROWS), ROWS)
+    lfin[p] = jnp.broadcast_to(colr[x, z][:, 1:2] - peak[z_rows, 0:1], (ROWS, 128))
+    for d in (4, 3, 5, 2, 6, 1, 7):
+        go(remote(lfin.at[p], lfin.at[p], ln_s.at[d - 1], ln_r.at[d - 1], dev_p(at_p(d))))
     grad_b = accb[x]
     for d in (1, 3, 2):
         remote(hb.at[x], hxb.at[d - 1], bx_s.at[d - 1], bx_r.at[d - 1], dev_x(d)).wait_recv()
@@ -400,14 +406,6 @@
     fin[p, :, cb] = grad_b.astype(BF16)
     for d in (4, 3, 5, 2, 6, 1, 7):
         go(remote(fin.at[p], fin.at[p], fn_s.at[d - 1], fn_r.at[d - 1], dev_p(at_p(d))))
-    for d in range(1, NZ):
-        remote(tsum, thz.at[d - 1], uz_s.at[d - 1], uz_r.at[d - 1], dev_z(d)).wait_recv()
-        told = told + thz[d - 1]
-    peak[0:128, :] = jnp.concatenate([told, jnp.zeros((120, 128), F32)], axis=0).T
-    z_rows = pl.ds(pl.multiple_of(z * ROWS, ROWS), ROWS)
-    lfin[p] = jnp.broadcast_to(colr[x, z][:, 1:2] - peak[z_rows, 0:1], (ROWS, 128))
-    for d in (4, 3, 5, 2, 6, 1, 7):
-        go(remote(lfin.at[p], lfin.at[p], ln_s.at[d - 1], ln_r.at[d - 1], dev_p(at_p(d))))
     for d in range(1, NP):
         src = at_p(NP - d)
         remote(lfin.at[p], lfin.at[src], ln_s.at[d - 1], ln_r.at[d - 1], dev_p(src)).wait_recv()
@@ -453,6 +451,8 @@
             vmem((NP, 1, CENT), F32),
             vmem((NP, QS, CENT), F32),
             vmem((NP, QS, CENT), BF16),
+            vmem((QS, 128), F32),
+            vmem((QS, 128), F32),
             vmem((QS, 128), F32),
             vmem((QS, 128), F32),
             vmem((QS, 128), F32),

time: 79.3 us -> 75.5 us (0.952)
  Pallas kernels: 78.5 us -> 74.7 us
    pallas_call x1, Pallas kernels: 76.8 us -> 73 us  [on_device(): pl.pallas_call(kernel, out_shape=(jax.ShapeDtypeStruct((1, CENT), F32), j...]
where the time goes in v5:
time: 75.5 us; the launch traced here: 75.4 us
  Pallas kernels  74.7 us (99%)
    pallas_call x1, Pallas kernels, on_device(): pl.pallas_call(kernel, out_shape=(jax.ShapeDtypeStruct((1, CENT), F32), j...  73 us
    pallas_call x1, Pallas kernels, on_device(): pl.pallas_call(finish, out_shape=(jax.ShapeDtypeStruct((1, CENT), F32), j...  1.72 us

profile of v5, /device:TPU:1, one launch (start us, length us, event | category | flops | bytes accessed | tf_op | source)
XLA Modules:
  0.0 75.4 jit_solution(13417640192314226182)
XLA Ops:
  0.6 73.0 %protonce.1 = (f32[1,512]{1,0:T(1,128)}, f32[8,16,128]{2,1,0:T(8,128)}, bf16[8,16,768]{2,1,0:T(8,128)(2,1)}) custom-call(bf16[512,768]{1,0:T(8,128)(2,1)} %cent.1, bf16[8,16,768]{2,1,0:T(8,128)(2,1)} %bitcast.12, bf16[8,4,8,16,768]{4,3,2,1,0:T(8,128)(2,1)} %bitcast.11, s32[8,16,32]{2,1,0:T(8,128)} %bitcast.13, s32[8,32]{1,0:T(8,128)} %bitcast.14, ...), custom_call_target="tpu_custom_call" | custom-call | tf_op jit(solution)/shard_map/protonce/pallas_call | solution.py:434
  73.6 1.7 %finish.1 = (f32[1,512]{1,0:T(1,128)}, f32[1,128]{1,0:T(1,128)}, bf16[128,768]{1,0:T(8,128)(2,1)}) custom-call(f32[1,512]{1,0:T(1,128)} %get-tuple-element.9.conc, f32[8,16,128]{2,1,0:T(8,128)} %get-tuple-element.10.lfin, bf16[8,16,768]{2,1,0:T(8,128)(2,1)} %get-tuple-element.11.fin), custom_call_target="tpu_custom_call" | custom-call | tf_op jit(solution)/shard_map/finish/pallas_call | solution.py:497

commit v6 on v5

--- a/solution.py
+++ b/solution.py
@@ -30,8 +30,8 @@
 
 
 def kernel(
-    cent, qry, mem, slot_in, count_in, pos_in, conc_o, lfin, fin,
-    call, qall, pall, mx, mall, slx, sall, invall, score, wgt, peak, sums, peakb, sumsb, hitw, hitz, tile, colr, posb, posw,
+    cent, qry, mem, slot_hbm, count_hbm, pos_hbm, conc_o, lfin, fin,
+    slot_in, count_in, pos_in, call, qall, pall, mx, mall, slx, sall, invall, score, wgt, peak, sums, peakb, sumsb, hitw, hitz, tile, colr, posb, posw,
     gsum, psum, slot, pos, tsend, trx, thz, tsum, ga, gra, ha, hza, acca, gb, grb, hb, hxb, accb,
     local, mx_s, mx_r, sx_s, sx_r, mz_s, mz_r, sz_s, sz_r, qz_s, qz_r, qx_s, qx_r, pz_s, pz_r, px_s, px_r,
     cy_s, cy_r, cc_s, cc_r, iv_s, iv_r, st_s, st_r, gx_s, gx_r, gz_s, gz_r, fn_s, fn_r, ln_s, ln_r,
@@ -78,8 +78,17 @@
     for q in (up, down, mate):
         pl.semaphore_signal(barrier, inc=1, device_id=dev_p(q), device_id_type=MESH)
 
+    loads = (
+        pltpu.make_async_copy(slot_hbm.at[p], slot_in, local.at[3]),
+        pltpu.make_async_copy(count_hbm, count_in, local.at[4]),
+        pltpu.make_async_copy(pos_hbm, pos_in, local.at[5]),
+    )
+    for copy in loads:
+        copy.start()
+    for copy in loads:
+        copy.wait()
     used = lax.broadcasted_iota(jnp.int32, (ROWS, NX * NZ), 0) < count_in[pl.ds(p, 1), :]
-    ids = jnp.where(used, slot_in[p], -1).astype(F32)
+    ids = jnp.where(used, slot_in[...], -1).astype(F32)
     ids = jnp.concatenate([ids, jnp.zeros((ROWS, 128 - NX * NZ), F32)], axis=1)
     ids = jnp.concatenate([ids, jnp.zeros((128 - ROWS, 128), F32)], axis=0).T
     for i in range(NX * NZ):
@@ -434,13 +443,16 @@
     conc, lfin, fin = pl.pallas_call(
         kernel,
         out_shape=(
-            jax.ShapeDtypeStruct((1, CENT), F32),
-            jax.ShapeDtypeStruct((NP, ROWS, 128), F32),
-            jax.ShapeDtypeStruct((NP, ROWS, WIDTH), BF16),
+            vmem((1, CENT), F32),
+            vmem((NP, ROWS, 128), F32),
+            vmem((NP, ROWS, WIDTH), BF16),
         ),
-        in_specs=[pl.BlockSpec(memory_space=pl.ANY)] * 3 + [whole] * 3,
+        in_specs=[pl.BlockSpec(memory_space=pl.ANY)] * 6,
         out_specs=(whole,) * 3,
         scratch_shapes=[
+            vmem((ROWS, NX * NZ), jnp.int32),
+            vmem((NP, NX * NZ), jnp.int32),
+            vmem((1, NP * ROWS), jnp.int32),
             vmem((NP, CENT, WIDTH), BF16),
             vmem((NX, NZ, ROWS, WIDTH), BF16),
             vmem((NX, NZ, 1, 128), F32),
@@ -479,7 +491,7 @@
             vmem((NX, ROWS, CB), BF16),
             vmem((NX - 1, ROWS, CB), BF16),
             vmem((NX, ROWS, CB), F32),
-            dma((3,)),
+            dma((6,)),
             *sems,
         ],
         compiler_params=pltpu.CompilerParams(
@@ -504,7 +516,7 @@
         in_specs=[whole] * 3,
         out_specs=(whole,) * 3,
         name="finish",
-    )(conc, lfin, fin)
+    )(*(pltpu.with_memory_space_constraint(v, vmem) for v in (conc, lfin, fin)))
     return conc.reshape(CENT), loss.reshape(NP * ROWS), grad
 
 

time: 75.5 us -> 73 us (0.967)
  Pallas kernels: 74.7 us -> 72.2 us
    pallas_call x1, Pallas kernels: 73 us -> 71.5 us  [on_device(): pl.pallas_call(kernel, out_shape=(vmem((1, CENT), F32), vmem((NP, ROWS, 1...]
    pallas_call x1, Pallas kernels: 1.72 us -> 0.75 us  [on_device(): pl.pallas_call(finish, out_shape=(jax.ShapeDtypeStruct((1, CENT), F32), j...]
where the time goes in v6:
time: 73 us; the launch traced here: 72.9 us
  Pallas kernels  72.2 us (99%)
    pallas_call x1, Pallas kernels, on_device(): pl.pallas_call(kernel, out_shape=(vmem((1, CENT), F32), vmem((NP, ROWS, 1...  71.5 us

profile of v6, /device:TPU:1, one launch (start us, length us, event | category | flops | bytes accessed | tf_op | source)
XLA Modules:
  0.0 72.9 jit_solution(12508869408855251590)
XLA Ops:
  0.6 71.5 %protonce.1 = (f32[1,512]{1,0:T(1,128)S(1)}, f32[8,16,128]{2,1,0:T(8,128)S(1)}, bf16[8,16,768]{2,1,0:T(8,128)(2,1)S(1)}) custom-call(bf16[512,768]{1,0:T(8,128)(2,1)} %cent.1, bf16[8,16,768]{2,1,0:T(8,128)(2,1)} %bitcast.12, bf16[8,4,8,16,768]{4,3,2,1,0:T(8,128)(2,1)} %bitcast.11, s32[8,16,32]{2,1,0:T(8,128)} %bitcast.13, s32[8,32]{1,0:T(8,128)} %bitcast.14, ...), custom_call_target="tpu_custom_call" | custom-call | tf_op jit(solution)/shard_map/protonce/pallas_call | solution.py:443
  72.1 0.8 %finish.1 = (f32[1,512]{1,0:T(1,128)}, f32[1,128]{1,0:T(1,128)}, bf16[128,768]{1,0:T(8,128)(2,1)}) custom-call(f32[1,512]{1,0:T(1,128)S(1)} %get-tuple-element.9.conc, f32[8,16,128]{2,1,0:T(8,128)S(1)} %get-tuple-element.10.lfin, bf16[8,16,768]{2,1,0:T(8,128)(2,1)S(1)} %get-tuple-element.11.fin), custom_call_target="tpu_custom_call" | custom-call | tf_op jit(solution)/shard_map/finish/pallas_call | solution.py:509

commit v7 on v6

--- a/solution.py
+++ b/solution.py
@@ -266,7 +266,7 @@
             peak[r, :] = fold(best, jnp.maximum)
             return carry
 
-        lax.fori_loop(0, QS // step, largest, 0)
+        lax.fori_loop(0, QS // step, largest, 0, unroll=4)
         peak[...] = jnp.broadcast_to(jnp.max(peak[...], axis=1, keepdims=True), (QS, 128))
 
         def soft(i, carry):
@@ -280,7 +280,7 @@
             sums[r, :] = fold(added, jnp.add)
             return carry
 
-        lax.fori_loop(0, QS // step, soft, 0)
+        lax.fori_loop(0, QS // step, soft, 0, unroll=4)
 
     early = (p, mate, down, up, down + flip, up + flip, far)
     last = far + flip
@@ -411,10 +411,14 @@
         remote(ha.at[z], hza.at[d - 1], gz_s.at[d - 1], gz_r.at[d - 1], dev_z(d)).wait_recv()
         grad_a = grad_a + hza[d - 1].astype(F32)
 
+    earlier = tuple(sends)
+    sends.clear()
     fin[p, :, ca] = grad_a.astype(BF16)
     fin[p, :, cb] = grad_b.astype(BF16)
     for d in (4, 3, 5, 2, 6, 1, 7):
         go(remote(fin.at[p], fin.at[p], fn_s.at[d - 1], fn_r.at[d - 1], dev_p(at_p(d))))
+    for copy in earlier:
+        copy.wait_send()
     for d in range(1, NP):
         src = at_p(NP - d)
         remote(lfin.at[p], lfin.at[src], ln_s.at[d - 1], ln_r.at[d - 1], dev_p(src)).wait_recv()

time: 73 us -> 72 us (0.986)
  Pallas kernels: 72.2 us -> 71.2 us
    pallas_call x1, Pallas kernels: 71.5 us -> 70.4 us  [on_device(): pl.pallas_call(kernel, out_shape=(vmem((1, CENT), F32), vmem((NP, ROWS, 1...]
where the time goes in v7:
time: 72 us; the launch traced here: 71.8 us
  Pallas kernels  71.2 us (99%)
    pallas_call x1, Pallas kernels, on_device(): pl.pallas_call(kernel, out_shape=(vmem((1, CENT), F32), vmem((NP, ROWS, 1...  70.4 us

profile of v7, /device:TPU:1, one launch (start us, length us, event | category | flops | bytes accessed | tf_op | source)
XLA Modules:
  0.0 71.8 jit_solution(17028027011717831121)
XLA Ops:
  0.6 70.4 %protonce.1 = (f32[1,512]{1,0:T(1,128)S(1)}, f32[8,16,128]{2,1,0:T(8,128)S(1)}, bf16[8,16,768]{2,1,0:T(8,128)(2,1)S(1)}) custom-call(bf16[512,768]{1,0:T(8,128)(2,1)} %cent.1, bf16[8,16,768]{2,1,0:T(8,128)(2,1)} %bitcast.12, bf16[8,4,8,16,768]{4,3,2,1,0:T(8,128)(2,1)} %bitcast.11, s32[8,16,32]{2,1,0:T(8,128)} %bitcast.13, s32[8,32]{1,0:T(8,128)} %bitcast.14, ...), custom_call_target="tpu_custom_call" | custom-call | tf_op jit(solution)/shard_map/protonce/pallas_call | solution.py:447
  71.1 0.8 %finish.1 = (f32[1,512]{1,0:T(1,128)}, f32[1,128]{1,0:T(1,128)}, bf16[128,768]{1,0:T(8,128)(2,1)}) custom-call(f32[1,512]{1,0:T(1,128)S(1)} %get-tuple-element.9.conc, f32[8,16,128]{2,1,0:T(8,128)S(1)} %get-tuple-element.10.lfin, bf16[8,16,768]{2,1,0:T(8,128)(2,1)S(1)} %get-tuple-element.11.fin), custom_call_target="tpu_custom_call" | custom-call | tf_op jit(solution)/shard_map/finish/pallas_call | solution.py:513

commit v8 on v7

--- a/solution.py
+++ b/solution.py
@@ -210,10 +210,8 @@
     scores(up)
     remote(call.at[down, top], call.at[down + flip, top], cc_s.at[1], cc_r.at[1], dev_p(mate)).wait_recv()
     remote(call.at[down, bottom], call.at[down + flip, bottom], cc_s.at[3], cc_r.at[3], dev_p(mate)).wait_recv()
-    scores(down + flip)
     remote(call.at[up, bottom], call.at[up + flip, bottom], cc_s.at[2], cc_r.at[2], dev_p(mate)).wait_recv()
     remote(call.at[up, top], call.at[up + flip, top], cc_s.at[4], cc_r.at[4], dev_p(mate)).wait_recv()
-    scores(up + flip)
 
     own[2].wait()
     for e in range(1, NZ):
@@ -235,6 +233,8 @@
     for d in (4, 3, 5, 2, 6, 1, 7):
         go(remote(invall.at[p], invall.at[p], iv_s.at[d - 1], iv_r.at[d - 1], dev_p(at_p(d))))
 
+    scores(down + flip)
+    scores(up + flip)
     positives(down)
     positives(up)
     positives(down + flip)

time: 72 us -> 71.6 us (level)
  no operation moved by 1% of the time
where the time goes in v8:
time: 71.6 us; the launch traced here: 71.4 us
  Pallas kernels  70.8 us (99%)
    pallas_call x1, Pallas kernels, on_device(): pl.pallas_call(kernel, out_shape=(vmem((1, CENT), F32), vmem((NP, ROWS, 1...  70 us

profile of v8, /device:TPU:1, one launch (start us, length us, event | category | flops | bytes accessed | tf_op | source)
XLA Modules:
  0.0 71.4 jit_solution(13061404658511277191)
XLA Ops:
  0.6 70.0 %protonce.1 = (f32[1,512]{1,0:T(1,128)S(1)}, f32[8,16,128]{2,1,0:T(8,128)S(1)}, bf16[8,16,768]{2,1,0:T(8,128)(2,1)S(1)}) custom-call(bf16[512,768]{1,0:T(8,128)(2,1)} %cent.1, bf16[8,16,768]{2,1,0:T(8,128)(2,1)} %bitcast.12, bf16[8,4,8,16,768]{4,3,2,1,0:T(8,128)(2,1)} %bitcast.11, s32[8,16,32]{2,1,0:T(8,128)} %bitcast.13, s32[8,32]{1,0:T(8,128)} %bitcast.14, ...), custom_call_target="tpu_custom_call" | custom-call | tf_op jit(solution)/shard_map/protonce/pallas_call | solution.py:447
  70.7 0.8 %finish.1 = (f32[1,512]{1,0:T(1,128)}, f32[1,128]{1,0:T(1,128)}, bf16[128,768]{1,0:T(8,128)(2,1)}) custom-call(f32[1,512]{1,0:T(1,128)S(1)} %get-tuple-element.9.conc, f32[8,16,128]{2,1,0:T(8,128)S(1)} %get-tuple-element.10.lfin, bf16[8,16,768]{2,1,0:T(8,128)(2,1)S(1)} %get-tuple-element.11.fin), custom_call_target="tpu_custom_call" | custom-call | tf_op jit(solution)/shard_map/finish/pallas_call | solution.py:513
